TPU v7x, 256 devices: a whole 4x4x8 slice. The times are simulated.
256 devices in a mesh: dp: 32 (over y, z_hi, core), expert: 8 (over x, z_lo).
Axes of the slice: x: 4, y: 4, z: 8 (z_hi: 4, z_lo: 2; z = z_hi * 2 + z_lo), core: 2. Of those that a mesh axis runs over, the one named last changes fastest.
Arguments:
- tokens: bfloat16 [4096, 3072], P('dp', 'expert'), may hold values from -6 to 6
- out_grad: bfloat16 [4096, 3072], P('dp', 'expert'), may hold values from -6 to 6
- expert_ids: int32 [4096, 2], P('dp'), may hold values from 0 to 7, all different within a row; in each aligned block of 128 rows (0 to 127, 128 to 255, ...) at most 33 rows name the same one
- route_weights: float32 [4096, 2], P('dp'), may hold values from 0.2 to 1
- w_gate: bfloat16 [8, 3072, 8192], P('expert', None, 'dp'), may hold values from -0.109375 to 0.109375
- w_up: bfloat16 [8, 3072, 8192], P('expert', None, 'dp'), may hold values from -0.109375 to 0.109375
- w_down: bfloat16 [8, 8192, 3072], P('expert', 'dp'), may hold values from -0.0625 to 0.0625
Outputs:
- combined: bfloat16 [4096, 3072], P('dp', 'expert')
- d_gate: bfloat16 [8, 3072, 8192], P('expert', None, 'dp')
- d_up: bfloat16 [8, 3072, 8192], P('expert', None, 'dp')
- d_down: bfloat16 [8, 8192, 3072], P('expert', 'dp')
- d_route: float32 [4096, 2], P('dp')
Inputs may be any that keep to these rules, and one draw needn't show every extreme that they name: `expert_ids`: each token names 2 different experts; among the 128 tokens of one index of dp no expert is named more than 33 times, a bound that some block reaches.
All inputs are finite; a program needn't handle non-finite values.
Results may differ from a plain program's by a relative error of at most 0.02.
Values may be sent and summed in bfloat16 or wider, within the bound.
A program may use at most 128 MiB of HBM per device.

v0:
```python
import jax
import jax.numpy as jnp
from jax import lax
from jax.sharding import PartitionSpec as P

highest = lax.Precision.HIGHEST


def slot_table(routed, experts):
    flattened = routed.reshape(-1)
    onehot = (flattened[:, None] == jnp.arange(experts, dtype=jnp.int32)[None, :]).astype(jnp.int32)
    before = jnp.cumsum(onehot, axis=0) - onehot
    return jnp.sum(before * onehot, axis=1).reshape(routed.shape)


def pick_tables(routed, experts, capacity):
    places = slot_table(routed, experts)
    target = routed * capacity + places
    row_ids = jnp.arange(experts * capacity, dtype=jnp.int32)[:, None]
    return [
        (row_ids == target[None, :, which]).astype(jnp.float32) for which in range(routed.shape[1])
    ]


def forward_rows(gathered, gate_slab, up_slab, down_slab):
    gate_pre = jnp.dot(gathered, gate_slab, preferred_element_type=jnp.float32)
    up_pre = jnp.dot(gathered, up_slab, preferred_element_type=jnp.float32)
    sigmoid_gate = jax.nn.sigmoid(gate_pre)
    hidden = (gate_pre * sigmoid_gate * up_pre).astype(jnp.bfloat16)
    partial_out = jnp.dot(hidden, down_slab, preferred_element_type=jnp.float32).astype(
        jnp.bfloat16
    )
    return ((gate_pre, up_pre, sigmoid_gate, hidden), partial_out)


def backward_rows(gathered, grads_in, saved, down_slab):
    gate_pre, up_pre, sigmoid_gate, hidden = saved
    d_hidden = jnp.einsum("rd,fd->rf", grads_in, down_slab, preferred_element_type=jnp.float32)
    d_down = jnp.einsum("rf,rd->fd", hidden, grads_in, preferred_element_type=jnp.float32).astype(
        jnp.bfloat16
    )
    d_gate_act = (
        d_hidden * up_pre * sigmoid_gate * (1.0 + gate_pre * (1.0 - sigmoid_gate))
    ).astype(jnp.bfloat16)
    d_up_act = (d_hidden * gate_pre * sigmoid_gate).astype(jnp.bfloat16)
    d_gate = jnp.einsum(
        "rd,rf->df", gathered, d_gate_act, preferred_element_type=jnp.float32
    ).astype(jnp.bfloat16)
    d_up = jnp.einsum("rd,rf->df", gathered, d_up_act, preferred_element_type=jnp.float32).astype(
        jnp.bfloat16
    )
    return (d_gate, d_up, d_down)


def return_rows(partial_out):
    summed_out = lax.psum_scatter(
        partial_out.astype(jnp.float32).astype(jnp.bfloat16), "dp", scatter_dimension=0, tiled=True
    )
    return lax.all_to_all(summed_out[None], "expert", split_axis=2, concat_axis=0, tiled=True)


def local(tokens, out_grad, expert_ids, route_weights, w_gate, w_up, w_down):
    experts = lax.axis_size("expert")
    tok_rows = tokens.shape[0]
    top_count = expert_ids.shape[1]
    capacity = min(tok_rows, tok_rows * top_count * 33 // (32 * experts))
    picks = pick_tables(expert_ids, experts, capacity)
    dispatch = sum(picks)
    weighted = sum((picks[which] * route_weights[None, :, which] for which in range(top_count)))
    sent_tokens = jnp.dot(dispatch.astype(jnp.bfloat16), tokens, preferred_element_type=jnp.float32)
    sent_tokens = sent_tokens.astype(jnp.bfloat16).reshape(experts, capacity, tokens.shape[1])
    sent_grads = jnp.dot(weighted, out_grad.astype(jnp.float32), precision=highest)
    sent_grads = sent_grads.astype(jnp.bfloat16).reshape(experts, capacity, tokens.shape[1])
    gate_slab = w_gate[0]
    up_slab = w_up[0]
    down_slab = w_down[0]
    recv_tokens, recv_grads = (
        lax.all_to_all(sent_tokens, "expert", split_axis=0, concat_axis=2, tiled=True),
        lax.all_to_all(sent_grads, "expert", split_axis=0, concat_axis=2, tiled=True),
    )
    gathered, grads_in = (
        lax.all_gather(recv_tokens[0], "dp", axis=0, tiled=True),
        lax.all_gather(recv_grads[0], "dp", axis=0, tiled=True),
    )
    saved, partial_out = forward_rows(gathered, gate_slab, up_slab, down_slab)
    d_gate, d_up, d_down = backward_rows(gathered, grads_in, saved, down_slab)
    returned_out = return_rows(partial_out)
    flat_out = returned_out.reshape(experts * capacity, -1).astype(jnp.float32)
    combined = jnp.dot(weighted.T, flat_out, precision=highest).astype(jnp.bfloat16)
    grads32 = out_grad.astype(jnp.float32)
    partial_dots = jnp.stack(
        [
            jnp.sum(grads32 * jnp.dot(picks[which].T, flat_out, precision=highest), axis=1)
            for which in range(top_count)
        ],
        axis=1,
    )
    d_route = lax.psum(partial_dots, "expert")
    return (combined, d_gate[None], d_up[None], d_down[None], d_route)


def solution(mesh):
    return jax.shard_map(
        local,
        mesh=mesh,
        in_specs=(
            P("dp", "expert"),
            P("dp", "expert"),
            P("dp", None),
            P("dp", None),
            P("expert", None, "dp"),
            P("expert", None, "dp"),
            P("expert", "dp", None),
        ),
        out_specs=(
            P("dp", "expert"),
            P("expert", None, "dp"),
            P("expert", None, "dp"),
            P("expert", "dp", None),
            P("dp", None),
        ),
        check_vma=False,
    )
```

profile of v0, /device:TPU:2, one launch (start us, length us, event | category | flops | bytes accessed | tf_op | source)
XLA Modules:
  0.0 383.3 jit_solution(13732426741167400095)
XLA Ops:
  7.2 0.9 copy.43
  8.1 0.1 eq.60
  8.3 0.1 eq.56
  8.4 0.6 reduce-window.6
  9.0 0.2 slice_reduce_fusion
  9.4 0.1 reshape.47
  9.6 0.7 multiply_add_fusion
  10.3 1.1 convolution_convert_fusion.5
  11.5 11.6 %all_to_all.45 = bf16[8,33,384]{2,1,0:T(8,128)(2,1)S(1)} all-to-all(bf16[8,33,384]{2,1,0:T(8,128)(2,1)S(1)} %reshape.48), channel_id=1, replica_groups=mesh['dp'=32,'expert'=8] {'expert'}, dimensions={0} | all-to-all | bytes 405504 | tf_op jit(solution)/shard_map/all_to_all | solution.py:78
  23.1 0.8 reshape.51
  24.0 0.4 convolution_convert_fusion.4
  24.5 9.5 %all_to_all.46 = bf16[8,33,384]{2,1,0:T(8,128)(2,1)S(1)} all-to-all(bf16[8,33,384]{2,1,0:T(8,128)(2,1)S(1)} %reshape.50), channel_id=1, replica_groups=mesh['dp'=32,'expert'=8] {'expert'}, dimensions={0} | all-to-all | bytes 405504 | tf_op jit(solution)/shard_map/all_to_all | solution.py:79
  34.1 0.8 reshape.53
  34.9 0.6 dynamic-slice.4
  36.1 65.0 %all-gather.5.cloned.1.call-done = bf16[32,33,3072]{2,1,0:T(8,128)(2,1)} async-done(((bf16[1,33,3072]{2,1,0:T(8,128)(2,1)}), bf16[32,33,3072]{2,1,0:T(8,128)(2,1)}) %all-gather.5.cloned.1.call-update) | async-done | bytes 6488080 | tf_op jit(solution)/shard_map/all_gather | solution.py:82
  101.1 7.1 %reshape.52 = bf16[1056,3072]{1,0:T(8,128)(2,1)} reshape(bf16[32,33,3072]{2,1,0:T(8,128)(2,1)} %all-gather.5.cloned.1.call-done) | data formatting | bytes 12976128
  108.2 4.8 %fusion.9 = f32[1056,256]{1,0:T(8,128)S(1)} fusion(bf16[1056,3072]{1,0:T(8,128)(2,1)} %reshape.52, bf16[1,3072,256]{2,1,0:T(8,128)(2,1)S(1)} %copy-done.11), kind=kOutput, calls=%fused_computation.12 | convolution fusion | flops 1660944384 | bytes 9142272 | tf_op jit(solution)/shard_map/dot_general | solution.py:26
  113.1 0.3 copy-done.12
  113.3 2.9 multiply_convert_fusion.2
  116.3 0.8 copy-done.2
  117.1 4.6 %convolution_convert_fusion = bf16[1056,3072]{1,0:T(8,128)(2,1)} fusion(bf16[1056,256]{1,0:T(8,128)(2,1)S(1)} %get-tuple-element.9, bf16[1,256,3072]{2,1,0:T(8,128)(2,1)S(1)} %copy-done), kind=kOutput, calls=%fused_computation | convolution fusion | flops 1664188416 | bytes 8601600 | tf_op jit(solution)/shard_map/dot_general | solution.py:30
  121.7 136.3 %fusion = bf16[40,3072]{1,0:T(8,128)(2,1)S(1)} fusion(bf16[1056,3072]{1,0:T(8,128)(2,1)} %convolution_convert_fusion), kind=kCustom, calls=%all-reduce-scatter | all-reduce-scatter fusion | flops 3932161 | bytes 6734848
  258.1 1.9 collective-permute-start.4
  260.0 5.3 %collective-permute-start.3 = (bf16[40,3072]{1,0:T(8,128)(2,1)S(1)}, bf16[40,3072]{1,0:T(8,128)(2,1)S(1)}, u32[]{:S(2)}, u32[]{:S(2)}) collective-permute-start(bf16[40,3072]{1,0:T(8,128)(2,1)S(1)} %fusion), channel_id=1, source_target_pairs={{0,32},{8,40},{16,48},{24,56},{32,64},{40,72},{48,80},{56,88},{64,... | collective-permute-start | bytes 737288
  265.2 3.1 collective-permute-start.2
  268.3 4.0 %collective-permute-start.1 = (bf16[40,3072]{1,0:T(8,128)(2,1)S(1)}, bf16[40,3072]{1,0:T(8,128)(2,1)S(1)}, u32[]{:S(2)}, u32[]{:S(2)}) collective-permute-start(bf16[40,3072]{1,0:T(8,128)(2,1)S(1)} %fusion), channel_id=1, source_target_pairs={{0,16},{8,24},{16,32},{24,40},{32,48},{40,56},{48,64},{56,72},{64,... | collective-permute-start | bytes 737288
  272.4 7.2 %reshape.54 = bf16[1056,3072]{1,0:T(8,128)(2,1)} reshape(bf16[32,33,3072]{2,1,0:T(8,128)(2,1)} %all-gather.7.cloned.1.call-done) | data formatting | bytes 12976128
  279.6 4.9 %fusion.4 = f32[1056,256]{1,0:T(8,128)S(1)} fusion(bf16[1056,3072]{1,0:T(8,128)(2,1)} %reshape.54, bf16[1,256,3072]{2,1,0:T(8,128)(2,1)S(1)} %copy-done), kind=kOutput, calls=%fused_computation.7 | convolution fusion | flops 1660944384 | bytes 9142272 | tf_op jit(solution)/shard_map/rd,fd->rf/dot_general | solution.py:38
  284.4 5.3 %collective-permute-start.5 = (bf16[17,3072]{1,0:T(8,128)(2,1)S(1)}, bf16[17,3072]{1,0:T(8,128)(2,1)S(1)}, u32[]{:S(2)}, u32[]{:S(2)}) collective-permute-start(bf16[17,3072]{1,0:T(8,128)(2,1)S(1)} %slice.25), channel_id=1, source_target_pairs={{0,48},{8,56},{16,64},{24,72},{32,80},{40,88},{48,96},{56,104},{64... | collective-permute-start | bytes 313352
  289.8 6.6 %fusion.1 = bf16[1,3072,256]{2,1,0:T(8,128)(2,1)} fusion(bf16[1056,3072]{1,0:T(8,128)(2,1)} %reshape.52, f32[1056,256]{1,0:T(8,128)S(1)} %copy-done.15, f32[1056,256]{1,0:T(8,128)S(1)} %fusion.4, f32[1056,256]{1,0:T(8,128)S(1)} %copy-done.16), kind=kOutput, calls=%fused_computation.4 | convolution fusion | flops 1664434176 | bytes 11304960 | tf_op jit(solution)/shard_map/rd,rf->df/dot_general | solution.py:46
  296.4 4.9 %collective-permute-start = (bf16[40,3072]{1,0:T(8,128)(2,1)S(1)}, bf16[40,3072]{1,0:T(8,128)(2,1)}, u32[]{:S(2)}, u32[]{:S(2)}) collective-permute-start(bf16[40,3072]{1,0:T(8,128)(2,1)S(1)} %fusion), channel_id=1, source_target_pairs={{0,8},{8,16},{16,24},{24,32},{32,40},{40,48},{48,56},{56,64},{64,7... | collective-permute-start | bytes 737288
  301.3 3.5 fusion.2
  304.9 0.6 copy-done.4
  305.5 0.1 copy-done.5
  305.7 0.7 copy-done.7
  306.4 11.9 %concatenate = bf16[257,3072]{1,0:T(8,128)(2,1)S(1)} concatenate(bf16[17,3072]{1,0:T(8,128)(2,1)} %copy-done.8, bf16[40,3072]{1,0:T(8,128)(2,1)} %copy-done.4, bf16[40,3072]{1,0:T(8,128)(2,1)} %copy-done.5, bf16[40,3072]{1,0:T(8,128)(2,1)} %copy-done.6, bf16[40,3072]{1,0:T(8,128)(2,1)} %copy-done.7, bf16[40,3072]{1,0:T(8,128)(2,1)} %collective-permute-done, bf16[40,3072]{1,0:T(8,128)(2,1)S(1)} %fusion), dimensions={0} | concatenate | bytes 3158016
  318.4 1.9 copy.47
  320.3 0.5 broadcast.45
  320.8 17.9 %reduce.2 = bf16[3072,33]{1,0:T(8,128)(2,1)} reduce(bf16[3072,1,33]{2,1,0:T(2,128)(2,1)S(1)} %bitcast.79, bf16[]{:T(256)} %broadcast.45), dimensions={1}, to_apply=%bitcast.60.reduce_sub_computation | reduce | bytes 405506
  338.7 3.1 reshape.59
  341.8 4.9 %all-to-all-start.1 = ((bf16[8,2,6336]{2,1,0:T(2,128)(2,1)}), bf16[8,2,6336]{2,1,0:T(2,128)(2,1)S(1)}, u32[]{:S(2)}, u32[]{:S(2)}) async-start(bf16[8,2,6336]{2,1,0:T(2,128)(2,1)} %reshape.59), calls=%async_computation.1 | async-start | bytes 409600 | tf_op jit(solution)/shard_map/all_to_all | solution.py:59
  346.7 6.2 %fusion.3 = bf16[1,256,3072]{2,1,0:T(8,128)(2,1)} fusion(bf16[1056,256]{1,0:T(8,128)(2,1)S(1)} %copy-done.3, bf16[1056,3072]{1,0:T(8,128)(2,1)} %reshape.54), kind=kOutput, calls=%fused_computation.6 | convolution fusion | flops 1661730816 | bytes 8601600 | tf_op jit(solution)/shard_map/rf,rd->fd/dot_general | solution.py:39
  353.0 1.8 reshape.60
  354.8 1.5 copy.48
  356.6 0.4 fusion.12
  356.9 0.4 fusion.11
  357.3 1.1 convolution_convert_fusion.6
  358.4 18.0 %psum.7 = f32[128,2]{0,1:T(2,128)} all-reduce(f32[128,2]{0,1:T(2,128)S(1)} %pad_maximum_fusion), channel_id=1, replica_groups=mesh['dp'=32,'expert'=8] {'expert'}, use_global_device_ids=true, to_apply=%region_6.7 | all-reduce | flops 256 | bytes 2048 | tf_op jit(solution)/shard_map/psum | solution.py:98
  (64 shorter events, 1.0 us)
Async XLA Ops:
  7.2 109.9 %copy-start = (bf16[1,256,3072]{2,1,0:T(8,128)(2,1)S(1)}, bf16[1,256,3072]{2,1,0:T(8,128)(2,1)}, u32[]{:S(2)}) copy-start(bf16[1,256,3072]{2,1,0:T(8,128)(2,1)} %param.13) | copy-start | bytes 4718596
  7.2 16.8 %copy-start.9 = (f32[128,2]{0,1:T(2,128)S(1)}, f32[128,2]{0,1:T(2,128)}, u32[]{:S(2)}) copy-start(f32[128,2]{0,1:T(2,128)} %param.10) | copy-start | bytes 3076
  7.2 16.8 %copy-start.13 = (bf16[128,384]{1,0:T(8,128)(2,1)S(1)}, bf16[128,384]{1,0:T(8,128)(2,1)}, u32[]{:S(2)}) copy-start(bf16[128,384]{1,0:T(8,128)(2,1)} %param.8) | copy-start | bytes 294916
  7.2 93.9 %all-gather.5.cloned.1.call-start = ((), (), s32[]{:S(2)}) async-start(), calls=%async_computation.3 | async-start | bytes 8110080 | tf_op jit(solution)/shard_map/all_gather | solution.py:82
  23.1 11.8 %copy-start.10 = (u32[256]{0:T(256)S(1)}, u32[256]{0:T(256)}, u32[]{:S(2)}) copy-start(u32[256]{0:T(256)} %constant.19) | copy-start | bytes 3076
  23.9 248.4 %all-gather.7.cloned.1.call-start = ((), (), s32[]{:S(2)}) async-start(), calls=%async_computation.4 | async-start | bytes 8110080 | tf_op jit(solution)/shard_map/all_gather | solution.py:83
  36.1 72.1 %copy-start.11 = (bf16[1,3072,256]{2,1,0:T(8,128)(2,1)S(1)}, bf16[1,3072,256]{2,1,0:T(8,128)(2,1)}, u32[]{:S(2)}) copy-start(bf16[1,3072,256]{2,1,0:T(8,128)(2,1)} %param.11) | copy-start | bytes 4718596
  108.2 4.9 %copy-start.1 = (bf16[1056,3072]{1,0:T(8,128)(2,1)S(1)}, bf16[1056,3072]{1,0:T(8,128)(2,1)}, u32[]{:S(2)}) copy-start(bf16[1056,3072]{1,0:T(8,128)(2,1)} %reshape.52) | copy-start | bytes 19464196
  108.2 5.1 %copy-start.12 = (bf16[1,3072,256]{2,1,0:T(8,128)(2,1)S(1)}, bf16[1,3072,256]{2,1,0:T(8,128)(2,1)}, u32[]{:S(2)}) copy-start(bf16[1,3072,256]{2,1,0:T(8,128)(2,1)} %param.12) | copy-start | bytes 4718596
  113.3 2.9 copy-start.14
  116.3 0.8 copy-start.2
  258.1 46.7 %collective-permute-start.4 = (bf16[40,3072]{1,0:T(8,128)(2,1)S(1)}, bf16[40,3072]{1,0:T(8,128)(2,1)S(1)}, u32[]{:S(2)}, u32[]{:S(2)}) collective-permute-start(bf16[40,3072]{1,0:T(8,128)(2,1)S(1)} %fusion), channel_id=1, source_target_pairs={{0,40},{8,48},{16,56},{24,64},{32,72},{40,80},{48,88},{56,96},{64,... | collective-permute-start | bytes 737288
  260.0 44.9 %collective-permute-start.3 = (bf16[40,3072]{1,0:T(8,128)(2,1)S(1)}, bf16[40,3072]{1,0:T(8,128)(2,1)S(1)}, u32[]{:S(2)}, u32[]{:S(2)}) collective-permute-start(bf16[40,3072]{1,0:T(8,128)(2,1)S(1)} %fusion), channel_id=1, source_target_pairs={{0,32},{8,40},{16,48},{24,56},{32,64},{40,72},{48,80},{56,88},{64,... | collective-permute-start | bytes 737288
  265.2 39.6 %collective-permute-start.2 = (bf16[40,3072]{1,0:T(8,128)(2,1)S(1)}, bf16[40,3072]{1,0:T(8,128)(2,1)S(1)}, u32[]{:S(2)}, u32[]{:S(2)}) collective-permute-start(bf16[40,3072]{1,0:T(8,128)(2,1)S(1)} %fusion), channel_id=1, source_target_pairs={{0,24},{8,32},{16,40},{24,48},{32,56},{40,64},{48,72},{56,80},{64,... | collective-permute-start | bytes 737288
  268.3 36.6 %collective-permute-start.1 = (bf16[40,3072]{1,0:T(8,128)(2,1)S(1)}, bf16[40,3072]{1,0:T(8,128)(2,1)S(1)}, u32[]{:S(2)}, u32[]{:S(2)}) collective-permute-start(bf16[40,3072]{1,0:T(8,128)(2,1)S(1)} %fusion), channel_id=1, source_target_pairs={{0,16},{8,24},{16,32},{24,40},{32,48},{40,56},{48,64},{56,72},{64,... | collective-permute-start | bytes 737288
  279.5 10.2 %copy-start.15 = (f32[1056,256]{1,0:T(8,128)S(1)}, f32[1056,256]{1,0:T(8,128)}, u32[]{:S(2)}) copy-start(f32[1056,256]{1,0:T(8,128)} %copy-done.14) | copy-start | bytes 3244036
  279.6 10.3 %copy-start.16 = (f32[1056,256]{1,0:T(8,128)S(1)}, f32[1056,256]{1,0:T(8,128)}, u32[]{:S(2)}) copy-start(f32[1056,256]{1,0:T(8,128)} %get-tuple-element.10) | copy-start | bytes 3244036
  279.6 21.8 %slice-start = ((s8[6488064]{0:T(1024)(128)(4,1)}), s8[4194304]{0:T(1024)(128)(4,1)S(1)}, s32[]{:S(2)}) async-start(s8[6488064]{0:T(1024)(128)(4,1)} %bitcast.77), calls=%async_computation.5 | async-start | bytes 8388608
  284.4 12.0 %collective-permute-start.5 = (bf16[17,3072]{1,0:T(8,128)(2,1)S(1)}, bf16[17,3072]{1,0:T(8,128)(2,1)S(1)}, u32[]{:S(2)}, u32[]{:S(2)}) collective-permute-start(bf16[17,3072]{1,0:T(8,128)(2,1)S(1)} %slice.25), channel_id=1, source_target_pairs={{0,48},{8,56},{16,64},{24,72},{32,80},{40,88},{48,96},{56,104},{64... | collective-permute-start | bytes 313352
  289.8 11.5 %slice-start.1 = ((s8[6488064]{0:T(1024)(128)(4,1)}), s8[2293760]{0:T(1024)(128)(4,1)S(1)}, s32[]{:S(2)}) async-start(s8[6488064]{0:T(1024)(128)(4,1)} %bitcast.77), calls=%async_computation.6 | async-start | bytes 4587520
  296.4 8.4 %copy-start.8 = (bf16[17,3072]{1,0:T(8,128)(2,1)}, bf16[17,3072]{1,0:T(8,128)(2,1)S(1)}, u32[]{:S(2)}) copy-start(bf16[17,3072]{1,0:T(8,128)(2,1)S(1)} %collective-permute-done.5) | copy-start | bytes 313348
  296.4 10.0 %collective-permute-start = (bf16[40,3072]{1,0:T(8,128)(2,1)S(1)}, bf16[40,3072]{1,0:T(8,128)(2,1)}, u32[]{:S(2)}, u32[]{:S(2)}) collective-permute-start(bf16[40,3072]{1,0:T(8,128)(2,1)S(1)} %fusion), channel_id=1, source_target_pairs={{0,8},{8,16},{16,24},{24,32},{32,40},{40,48},{48,56},{56,64},{64,7... | collective-permute-start | bytes 737288
  304.9 0.7 copy-start.4
  304.9 0.8 copy-start.5
  304.9 0.8 copy-start.6
  305.7 0.7 copy-start.7
  338.7 8.1 %copy-start.3 = (bf16[1056,256]{1,0:T(8,128)(2,1)S(1)}, bf16[1056,256]{1,0:T(8,128)(2,1)}, u32[]{:S(2)}) copy-start(bf16[1056,256]{1,0:T(8,128)(2,1)} %copy-done.2) | copy-start | bytes 1622020
  341.8 11.2 %all-to-all-start.1 = ((bf16[8,2,6336]{2,1,0:T(2,128)(2,1)}), bf16[8,2,6336]{2,1,0:T(2,128)(2,1)S(1)}, u32[]{:S(2)}, u32[]{:S(2)}) async-start(bf16[8,2,6336]{2,1,0:T(2,128)(2,1)} %reshape.59), calls=%async_computation.1 | async-start | bytes 409600 | tf_op jit(solution)/shard_map/all_to_all | solution.py:59
Sparse Core Ops, SparseCore 0:
  24.1 76.9 all-gather.4
  104.2 96.1 all-gather.6
where the time goes:
time: 391 us; the launch traced here: 383 us
  blocking collectives  175 us (45%)
  waiting for transfers between devices  65 us (17%)
  local copies, waits for them, and re-layouts  42 us (11%)
  matrix products  36.9 us (9%)
  starting transfers between devices  29.5 us (8%)
  other arithmetic  19.3 us (5%)
  between operations  15.1 us (4%)
    unnamed x1, blocking collectives  136 us
    all_gather x1, waiting for transfers between devices, local(): lax.all_gather(recv_tokens[0], 'dp', axis=0, tiled=True)  65 us
    unnamed x50, local copies, waits for them, and re-layouts  37.4 us
    unnamed x6, starting transfers between devices  24.5 us
    psum x1, blocking collectives, local(): d_route = lax.psum(partial_dots, 'expert')  18 us
    unnamed x2, other arithmetic  17.9 us
    all_to_all x1, blocking collectives, local(): lax.all_to_all(sent_tokens, 'expert', split_axis=0, concat_axis=2, tiled=...  11.6 us
    all_to_all x1, blocking collectives, local(): lax.all_to_all(sent_grads, 'expert', split_axis=0, concat_axis=2, tiled=T...  9.55 us
  transfers between devices with their start and end apart: 9, of which 1 were waited for; matrix products, arithmetic and copies ran while one was open for 49% of the time, Pallas kernels for 0%

commit v1 on v0

v1 whole, which is shorter than its diff:
```python
import jax
import jax.numpy as jnp
from jax import lax
from jax.sharding import Mesh
from jax.sharding import PartitionSpec as P

highest = lax.Precision.HIGHEST
DP = ("dpo", "core")


def slot_table(routed, experts):
    flattened = routed.reshape(-1)
    onehot = (flattened[:, None] == jnp.arange(experts, dtype=jnp.int32)[None, :]).astype(jnp.int32)
    before = jnp.cumsum(onehot, axis=0) - onehot
    return jnp.sum(before * onehot, axis=1).reshape(routed.shape)


def pick_tables(routed, experts, capacity):
    places = slot_table(routed, experts)
    target = routed * capacity + places
    row_ids = jnp.arange(experts * capacity, dtype=jnp.int32)[:, None]
    return [
        (row_ids == target[None, :, which]).astype(jnp.float32) for which in range(routed.shape[1])
    ]


def local(tokens, out_grad, expert_ids, route_weights, w_gate, w_up, w_down):
    experts = lax.axis_size("expert")
    n_core = lax.axis_size("core")
    tok_rows, feat = tokens.shape
    top_count = expert_ids.shape[1]
    capacity = min(tok_rows, tok_rows * top_count * 33 // (32 * experts))
    picks = pick_tables(expert_ids, experts, capacity)
    dispatch = sum(picks)
    weighted = sum((picks[which] * route_weights[None, :, which] for which in range(top_count)))
    sent_tokens = jnp.dot(dispatch.astype(jnp.bfloat16), tokens, preferred_element_type=jnp.float32)
    sent_tokens = sent_tokens.astype(jnp.bfloat16).reshape(experts, 1, capacity, feat)
    sent_grads = jnp.dot(weighted, out_grad.astype(jnp.float32), precision=highest)
    sent_grads = sent_grads.astype(jnp.bfloat16).reshape(experts, 1, capacity, feat)
    sent = jnp.concatenate([sent_tokens, sent_grads], axis=1)
    recv = lax.all_to_all(sent, "expert", split_axis=0, concat_axis=3, tiled=True)
    half = lax.all_gather(recv, "dpo", axis=0, tiled=True)
    full = lax.all_gather(half, "core", axis=0, tiled=True)
    n_rows = full.shape[0] * capacity
    d_all = full.shape[3]
    gathered = full[:, 0].reshape(n_rows, d_all)
    grads_in = full[:, 1].reshape(n_rows, d_all)
    gate_slab = w_gate[0]
    up_slab = w_up[0]
    down_slab = w_down[0]

    gate_pre = jnp.dot(gathered, gate_slab, preferred_element_type=jnp.float32)
    up_pre = jnp.dot(gathered, up_slab, preferred_element_type=jnp.float32)
    sigmoid_gate = jax.nn.sigmoid(gate_pre)
    hidden = (gate_pre * sigmoid_gate * up_pre).astype(jnp.bfloat16)
    partial_out = jnp.dot(hidden, down_slab, preferred_element_type=jnp.float32).astype(jnp.bfloat16)

    d_hidden = jnp.einsum("rd,fd->rf", grads_in, down_slab, preferred_element_type=jnp.float32)
    d_down = jnp.einsum("rf,rd->fd", hidden, grads_in, preferred_element_type=jnp.float32).astype(
        jnp.bfloat16
    )
    d_gate_act = (
        d_hidden * up_pre * sigmoid_gate * (1.0 + gate_pre * (1.0 - sigmoid_gate))
    ).astype(jnp.bfloat16)
    d_up_act = (d_hidden * gate_pre * sigmoid_gate).astype(jnp.bfloat16)
    d_gate = jnp.einsum(
        "rd,rf->df", gathered, d_gate_act, preferred_element_type=jnp.float32
    ).astype(jnp.bfloat16)
    d_up = jnp.einsum("rd,rf->df", gathered, d_up_act, preferred_element_type=jnp.float32).astype(
        jnp.bfloat16
    )

    blocks = partial_out.reshape(full.shape[0], capacity, d_all)
    on_chip = lax.psum_scatter(blocks, "core", scatter_dimension=0, tiled=True)
    summed_out = lax.psum_scatter(on_chip, "dpo", scatter_dimension=0, tiled=True)
    returned_out = lax.all_to_all(summed_out, "expert", split_axis=2, concat_axis=0, tiled=True)
    flat_out = returned_out.reshape(experts * capacity, -1).astype(jnp.float32)
    combined = jnp.dot(weighted.T, flat_out, precision=highest).astype(jnp.bfloat16)
    grads32 = out_grad.astype(jnp.float32)
    partial_dots = jnp.stack(
        [
            jnp.sum(grads32 * jnp.dot(picks[which].T, flat_out, precision=highest), axis=1)
            for which in range(top_count)
        ],
        axis=1,
    )
    d_route = lax.psum(partial_dots, "expert")
    return (combined, d_gate[None], d_up[None], d_down[None], d_route)


def solution(mesh):
    n_dp, n_exp = mesh.devices.shape
    split = Mesh(mesh.devices.reshape(n_dp // 2, 2, n_exp), ("dpo", "core", "expert"))
    return jax.shard_map(
        local,
        mesh=split,
        in_specs=(
            P(DP, "expert"),
            P(DP, "expert"),
            P(DP, None),
            P(DP, None),
            P("expert", None, DP),
            P("expert", None, DP),
            P("expert", DP, None),
        ),
        out_specs=(
            P(DP, "expert"),
            P("expert", None, DP),
            P("expert", None, DP),
            P("expert", DP, None),
            P(DP, None),
        ),
        check_vma=False,
    )
```

time: 391 us -> 445 us (1.14); the launches traced: 383 us -> 443 us
  waiting for transfers between devices: 65 us -> 234 us
  blocking collectives: 175 us -> 31.2 us
  local copies, waits for them, and re-layouts: 42 us -> 102 us
  starting transfers between devices: 29.5 us -> 4.97 us
    unnamed x1 -> x0, blocking collectives: 136 us -> none
    reduce_scatter x0 -> x2, waiting for transfers between devices: none -> 102 us  [the longest x1 78.3 us: local(): lax.psum_scatter(on_chip, 'dpo', scatter_dimension=0, tiled=True)]
    all_gather x2, waiting for transfers between devices: 65 us -> 132 us  [the longest x1 92.8 us: local(): half = lax.all_gather(recv, 'dpo', axis=0, tiled=True)]
    slice x1 -> x2, local copies, waits for them, and re-layouts: 0.21 us -> 65.4 us  [the longest x1 65.2 us: local(): grads_in = full[:, 1].reshape(n_rows, d_all)]
    unnamed x50 -> x27, local copies, waits for them, and re-layouts: 37.4 us -> 7.5 us
    unnamed x6 -> x0, starting transfers between devices: 24.5 us -> none
    another operation x1 -> x3, local copies, waits for them, and re-layouts: 0.01 us -> 14.6 us  [the longest x1 7.32 us: local(): grads_in = full[:, 1].reshape(n_rows, d_all)]
    all_to_all x2 -> x1, blocking collectives: 21.1 us -> 13.2 us  [local(): lax.all_to_all(sent, 'expert', split_axis=0, concat_axis=3, tiled=True)]
  transfers between devices with their start and end apart: 9 -> 5, of which waited for: 1 -> 4; matrix products, arithmetic and copies ran while one was open for 49% -> 6% of each run, Pallas kernels for 0% -> 0%
where the time goes in v1:
time: 445 us; the launch traced here: 443 us
  waiting for transfers between devices  234 us (53%)
  local copies, waits for them, and re-layouts  102 us (23%)
  matrix products  36.7 us (8%)
  blocking collectives  31.2 us (7%)
  other arithmetic  19.6 us (4%)
  between operations  14 us (3%)
  starting transfers between devices  4.97 us (1%)
    all_gather x1, waiting for transfers between devices, local(): half = lax.all_gather(recv, 'dpo', axis=0, tiled=True)  92.8 us
    reduce_scatter x1, waiting for transfers between devices, local(): lax.psum_scatter(on_chip, 'dpo', scatter_dimension=0, tiled=True)  78.3 us
    slice x1, local copies, waits for them, and re-layouts, local(): grads_in = full[:, 1].reshape(n_rows, d_all)  65.2 us
    all_gather x1, waiting for transfers between devices, local(): full = lax.all_gather(half, 'core', axis=0, tiled=True)  39.3 us
    reduce_scatter x1, waiting for transfers between devices, local(): on_chip = lax.psum_scatter(blocks, 'core', scatter_dimension=0, tiled=True)  23.7 us
    unnamed x2, other arithmetic  18.1 us
    psum x1, blocking collectives, local(): d_route = lax.psum(partial_dots, 'expert')  18 us
    all_to_all x1, blocking collectives, local(): lax.all_to_all(sent, 'expert', split_axis=0, concat_axis=3, tiled=True)  13.2 us
  transfers between devices with their start and end apart: 5, of which 4 were waited for; matrix products, arithmetic and copies ran while one was open for 6% of the time, Pallas kernels for 0%

profile of v1, /device:TPU:2, one launch (start us, length us, event | category | flops | bytes accessed | tf_op | source)
XLA Modules:
  0.0 443.1 jit_solution(14833741383290562498)
XLA Ops:
  7.2 0.9 copy.41
  8.1 0.1 eq.60
  8.3 0.1 eq.56
  8.4 0.8 slice_bitcast_fusion.2
  9.2 0.6 reduce-window.6
  9.7 0.2 slice_reduce_fusion.2
  10.0 0.1 fusion.29
  10.1 0.1 reshape.48
  10.2 0.1 copy.43
  10.3 0.7 multiply_add_fusion
  11.0 1.1 convolution_convert_fusion.5
  12.1 0.1 reshape.49
  12.2 1.3 convolution_convert_fusion.4
  13.5 0.1 reshape.50
  13.6 0.1 pad_maximum_fusion
  13.6 0.4 copy.44
  14.1 13.2 %all_to_all.33 = bf16[8,2,33,384]{3,1,2,0:T(2,128)(2,1)S(1)} all-to-all(bf16[8,2,33,384]{3,1,2,0:T(2,128)(2,1)S(1)} %copy.44), channel_id=1, replica_groups=mesh['dpo'=16,'core'=2,'expert'=8] {'expert'}, dimensions={0} | all-to-all | bytes 811008 | tf_op jit(solution)/shard_map/all_to_all | solution.py:41
  27.3 1.0 copy.51
  28.4 92.8 %all-gather.3.cloned.1.call-done = bf16[16,2,33,3072]{3,1,2,0:T(2,128)(2,1)} async-done(((bf16[1,2,33,3072]{3,1,2,0:T(2,128)(2,1)}), bf16[16,2,33,3072]{3,1,2,0:T(2,128)(2,1)}) %all-gather.3.cloned.1.call-update) | async-done | bytes 6488080 | tf_op jit(solution)/shard_map/all_gather | solution.py:42
  121.3 39.3 %all-gather.5.cloned.1.call-done = bf16[32,2,33,3072]{3,1,2,0:T(2,128)(2,1)} async-done(((bf16[16,2,33,3072]{3,1,2,0:T(2,128)(2,1)}), bf16[32,2,33,3072]{3,1,2,0:T(2,128)(2,1)}) %all-gather.5.cloned.1.call-update) | async-done | bytes 12976144 | tf_op jit(solution)/shard_map/all_gather | solution.py:43
  160.5 65.2 %slice_reduce_fusion = (bf16[32,33,3072]{2,1,0:T(8,128)(2,1)}, bf16[32,33,3072]{2,1,0:T(8,128)(2,1)}) fusion(bf16[32,2,33,3072]{3,1,2,0:T(2,128)(2,1)} %all-gather.5.cloned.1.call-done), kind=kLoop, calls=%fused_computation | loop fusion | bytes 25952256 | tf_op jit(solution)/shard_map/slice | solution.py:47
  225.7 7.2 %reshape_squeeze.6 = bf16[1056,3072]{1,0:T(8,128)(2,1)} reshape(bf16[32,33,3072]{2,1,0:T(8,128)(2,1)} %get-tuple-element.6) | data formatting | bytes 12976128 | tf_op jit(solution)/shard_map/reshape;squeeze | solution.py:46
  232.9 4.8 %fusion.8 = f32[1056,256]{1,0:T(8,128)S(1)} fusion(bf16[1056,3072]{1,0:T(8,128)(2,1)} %reshape_squeeze.6, bf16[1,3072,256]{2,1,0:T(8,128)(2,1)S(1)} %copy-done.4), kind=kOutput, calls=%fused_computation.14 | convolution fusion | flops 1660944384 | bytes 9142272 | tf_op jit(solution)/shard_map/dot_general | solution.py:52
  237.8 0.3 copy-done.5
  238.1 2.0 multiply_convert_fusion.2
  240.0 0.8 copy-done.2
  240.8 4.5 %convolution_convert_fusion = bf16[1056,3072]{1,0:T(8,128)(2,1)} fusion(bf16[1056,256]{1,0:T(8,128)(2,1)S(1)} %get-tuple-element.11, bf16[1,256,3072]{2,1,0:T(8,128)(2,1)S(1)} %copy-done), kind=kOutput, calls=%fused_computation.2 | convolution fusion | flops 1664188416 | bytes 8601600 | tf_op jit(solution)/shard_map/dot_general | solution.py:56
  245.3 7.1 %reshape.51 = bf16[32,33,3072]{2,1,0:T(8,128)(2,1)} reshape(bf16[1056,3072]{1,0:T(8,128)(2,1)} %convolution_convert_fusion) | data formatting | bytes 12976128 | tf_op jit(solution)/shard_map/reshape | solution.py:73
  252.5 0.0 reduce-scatter.5.cloned.1.call-start
  252.5 23.7 %reduce-scatter.3.cloned.1.call-done = bf16[16,33,3072]{2,1,0:T(8,128)(2,1)} async-done(((bf16[32,33,3072]{2,1,0:T(8,128)(2,1)}), bf16[16,33,3072]{2,1,0:T(8,128)(2,1)}) %reduce-scatter.3.cloned.1.call-update) | async-done | bytes 3244048 | tf_op jit(solution)/shard_map/reduce_scatter | solution.py:74
  276.2 7.3 %reshape_squeeze.7 = bf16[1056,3072]{1,0:T(8,128)(2,1)} reshape(bf16[32,33,3072]{2,1,0:T(8,128)(2,1)} %get-tuple-element.5) | data formatting | bytes 12976128 | tf_op jit(solution)/shard_map/reshape;squeeze | solution.py:47
  283.5 4.9 %fusion.3 = f32[1056,256]{1,0:T(8,128)S(1)} fusion(bf16[1056,3072]{1,0:T(8,128)(2,1)} %reshape_squeeze.7, bf16[1,256,3072]{2,1,0:T(8,128)(2,1)S(1)} %copy-done), kind=kOutput, calls=%fused_computation.9 | convolution fusion | flops 1660944384 | bytes 9142272 | tf_op jit(solution)/shard_map/rd,fd->rf/dot_general | solution.py:58
  288.4 6.5 %fusion.1 = bf16[1,3072,256]{2,1,0:T(8,128)(2,1)} fusion(bf16[1056,3072]{1,0:T(8,128)(2,1)} %reshape_squeeze.6, f32[1056,256]{1,0:T(8,128)S(1)} %fusion.3, f32[1056,256]{1,0:T(8,128)S(1)} %copy-done.8), kind=kOutput, calls=%fused_computation.7 | convolution fusion | flops 1663352832 | bytes 10223616 | tf_op jit(solution)/shard_map/rd,rf->df/dot_general | solution.py:69
  295.0 3.6 fusion
  298.6 78.3 %reduce-scatter.5.cloned.1.call-done = bf16[1,33,3072]{2,1,0:T(8,128)(2,1)} async-done(((bf16[16,33,3072]{2,1,0:T(8,128)(2,1)}), bf16[1,33,3072]{2,1,0:T(8,128)(2,1)}) %reduce-scatter.5.cloned.1.call-update) | async-done | bytes 202768 | tf_op jit(solution)/shard_map/reduce_scatter | solution.py:75
  376.9 3.4 copy.46
  380.3 0.5 broadcast.47
  380.8 18.1 %reduce.6 = bf16[3072,33]{1,0:T(8,128)(2,1)} reduce(bf16[3072,1,33]{2,1,0:T(2,128)(2,1)S(1)} %bitcast.69, bf16[]{:T(256)} %broadcast.47), dimensions={1}, to_apply=%bitcast.50.reduce_sub_computation | reduce | bytes 405506
  398.9 3.1 reshape.56
  402.0 4.8 %all-to-all-start.1 = ((bf16[8,2,6336]{2,1,0:T(2,128)(2,1)}), bf16[8,2,6336]{2,1,0:T(2,128)(2,1)S(1)}, u32[]{:S(2)}, u32[]{:S(2)}) async-start(bf16[8,2,6336]{2,1,0:T(2,128)(2,1)} %reshape.56), calls=%async_computation.3 | async-start | bytes 409600 | tf_op jit(solution)/shard_map/all_to_all | solution.py:76
  406.8 6.2 %fusion.2 = bf16[1,256,3072]{2,1,0:T(8,128)(2,1)} fusion(bf16[1056,256]{1,0:T(8,128)(2,1)S(1)} %copy-done.3, bf16[1056,3072]{1,0:T(8,128)(2,1)} %reshape_squeeze.7), kind=kOutput, calls=%fused_computation.8 | convolution fusion | flops 1661730816 | bytes 8601600 | tf_op jit(solution)/shard_map/rf,rd->fd/dot_general | solution.py:59
  413.1 1.8 reshape.57
  414.9 1.5 copy.47
  416.6 0.1 reshape.52
  416.7 0.4 fusion.11
  417.1 0.4 fusion.10
  417.4 1.1 convolution_convert_fusion.6
  418.5 18.0 %psum.7 = f32[128,2]{0,1:T(2,128)} all-reduce(f32[128,2]{0,1:T(2,128)S(1)} %pad_maximum_fusion.1), channel_id=1, replica_groups=mesh['dpo'=16,'core'=2,'expert'=8] {'expert'}, use_global_device_ids=true, to_apply=%region_7.8 | all-reduce | flops 256 | bytes 2048 | tf_op jit(solution)/shard_map/psum | solution.py:87
  (37 shorter events, 0.4 us)
Async XLA Ops:
  7.2 233.7 %copy-start = (bf16[1,256,3072]{2,1,0:T(8,128)(2,1)S(1)}, bf16[1,256,3072]{2,1,0:T(8,128)(2,1)}, u32[]{:S(2)}) copy-start(bf16[1,256,3072]{2,1,0:T(8,128)(2,1)} %param.13) | copy-start | bytes 4718596
  7.2 114.0 %all-gather.3.cloned.1.call-start = ((), (), s32[]{:S(2)}) async-start(), calls=%async_computation.4 | async-start | bytes 6893568 | tf_op jit(solution)/shard_map/all_gather | solution.py:42
  28.4 132.1 %all-gather.5.cloned.1.call-start = ((), (), s32[]{:S(2)}) async-start(), calls=%async_computation.5 | async-start | bytes 19464192 | tf_op jit(solution)/shard_map/all_gather | solution.py:43
  121.2 155.0 %reduce-scatter.3.cloned.1.call-start = ((), (), s32[]{:S(2)}) async-start(), calls=%async_computation.6 | async-start | bytes 11796480 | tf_op jit(solution)/shard_map/reduce_scatter | solution.py:74
  225.7 7.2 %copy-start.4 = (bf16[1,3072,256]{2,1,0:T(8,128)(2,1)S(1)}, bf16[1,3072,256]{2,1,0:T(8,128)(2,1)}, u32[]{:S(2)}) copy-start(bf16[1,3072,256]{2,1,0:T(8,128)(2,1)} %param.11) | copy-start | bytes 4718596
  232.9 4.9 %copy-start.1 = (bf16[1056,3072]{1,0:T(8,128)(2,1)S(1)}, bf16[1056,3072]{1,0:T(8,128)(2,1)}, u32[]{:S(2)}) copy-start(bf16[1056,3072]{1,0:T(8,128)(2,1)} %reshape_squeeze.6) | copy-start | bytes 19464196
  232.9 5.1 %copy-start.5 = (bf16[1,3072,256]{2,1,0:T(8,128)(2,1)S(1)}, bf16[1,3072,256]{2,1,0:T(8,128)(2,1)}, u32[]{:S(2)}) copy-start(bf16[1,3072,256]{2,1,0:T(8,128)(2,1)} %param.12) | copy-start | bytes 4718596
  238.1 2.0 copy-start.7
  240.0 0.8 copy-start.2
  252.5 124.4 %reduce-scatter.5.cloned.1.call-start = ((), (), s32[]{:S(2)}) async-start(), calls=%async_computation.7 | async-start | bytes 4177920 | tf_op jit(solution)/shard_map/reduce_scatter | solution.py:75
  283.5 4.9 %copy-start.8 = (f32[1056,256]{1,0:T(8,128)S(1)}, f32[1056,256]{1,0:T(8,128)}, u32[]{:S(2)}) copy-start(f32[1056,256]{1,0:T(8,128)} %copy-done.7) | copy-start | bytes 3244036
  283.5 11.4 %slice-start = ((s8[6488064]{0:T(1024)(128)(4,1)}), s8[4194304]{0:T(1024)(128)(4,1)S(1)}, s32[]{:S(2)}) async-start(s8[6488064]{0:T(1024)(128)(4,1)} %bitcast.67), calls=%async_computation.8 | async-start | bytes 8388608
  288.4 6.5 %slice-start.1 = ((s8[6488064]{0:T(1024)(128)(4,1)}), s8[2293760]{0:T(1024)(128)(4,1)S(1)}, s32[]{:S(2)}) async-start(s8[6488064]{0:T(1024)(128)(4,1)} %bitcast.67), calls=%async_computation.9 | async-start | bytes 4587520
  398.9 8.0 %copy-start.3 = (bf16[1056,256]{1,0:T(8,128)(2,1)S(1)}, bf16[1056,256]{1,0:T(8,128)(2,1)}, u32[]{:S(2)}) copy-start(bf16[1056,256]{1,0:T(8,128)(2,1)} %copy-done.2) | copy-start | bytes 1622020
  402.0 11.0 %all-to-all-start.1 = ((bf16[8,2,6336]{2,1,0:T(2,128)(2,1)}), bf16[8,2,6336]{2,1,0:T(2,128)(2,1)S(1)}, u32[]{:S(2)}, u32[]{:S(2)}) async-start(bf16[8,2,6336]{2,1,0:T(2,128)(2,1)} %reshape.56), calls=%async_computation.3 | async-start | bytes 409600 | tf_op jit(solution)/shard_map/all_to_all | solution.py:76
  414.9 1.8 copy-start.6
Sparse Core Ops, SparseCore 0:
  28.5 92.6 all-gather.2
  123.0 37.4 all-gather.4
  252.6 23.5 reduce-scatter.2
  279.7 97.1 reduce-scatter.4

commit v2 on v1

--- a/solution.py
+++ b/solution.py
@@ -34,17 +34,23 @@
     dispatch = sum(picks)
     weighted = sum((picks[which] * route_weights[None, :, which] for which in range(top_count)))
     sent_tokens = jnp.dot(dispatch.astype(jnp.bfloat16), tokens, preferred_element_type=jnp.float32)
-    sent_tokens = sent_tokens.astype(jnp.bfloat16).reshape(experts, 1, capacity, feat)
+    sent_tokens = sent_tokens.astype(jnp.bfloat16).reshape(1, experts, capacity, feat)
     sent_grads = jnp.dot(weighted, out_grad.astype(jnp.float32), precision=highest)
-    sent_grads = sent_grads.astype(jnp.bfloat16).reshape(experts, 1, capacity, feat)
-    sent = jnp.concatenate([sent_tokens, sent_grads], axis=1)
-    recv = lax.all_to_all(sent, "expert", split_axis=0, concat_axis=3, tiled=True)
-    half = lax.all_gather(recv, "dpo", axis=0, tiled=True)
-    full = lax.all_gather(half, "core", axis=0, tiled=True)
-    n_rows = full.shape[0] * capacity
-    d_all = full.shape[3]
-    gathered = full[:, 0].reshape(n_rows, d_all)
-    grads_in = full[:, 1].reshape(n_rows, d_all)
+    sent_grads = sent_grads.astype(jnp.bfloat16).reshape(1, experts, capacity, feat)
+    sent = jnp.concatenate([sent_tokens, sent_grads], axis=0)
+    recv = lax.all_to_all(sent, "expert", split_axis=1, concat_axis=3, tiled=True)
+
+    def gather(part):
+        half = lax.all_gather(part, "dpo", axis=0, tiled=True)
+        return lax.all_gather(half, "core", axis=0, tiled=True)
+
+    x_blocks = gather(recv[0])
+    g_blocks = gather(recv[1])
+    n_blk = x_blocks.shape[0]
+    d_all = x_blocks.shape[2]
+    n_rows = n_blk * capacity
+    gathered = x_blocks.reshape(n_rows, d_all)
+    grads_in = g_blocks.reshape(n_rows, d_all)
     gate_slab = w_gate[0]
     up_slab = w_up[0]
     down_slab = w_down[0]
@@ -70,10 +76,10 @@
         jnp.bfloat16
     )
 
-    blocks = partial_out.reshape(full.shape[0], capacity, d_all)
+    blocks = partial_out.reshape(n_blk, capacity, experts, d_all // experts).transpose(0, 2, 1, 3)
     on_chip = lax.psum_scatter(blocks, "core", scatter_dimension=0, tiled=True)
     summed_out = lax.psum_scatter(on_chip, "dpo", scatter_dimension=0, tiled=True)
-    returned_out = lax.all_to_all(summed_out, "expert", split_axis=2, concat_axis=0, tiled=True)
+    returned_out = lax.all_to_all(summed_out, "expert", split_axis=1, concat_axis=0, tiled=True)
     flat_out = returned_out.reshape(experts * capacity, -1).astype(jnp.float32)
     combined = jnp.dot(weighted.T, flat_out, precision=highest).astype(jnp.bfloat16)
     grads32 = out_grad.astype(jnp.float32)

time: 445 us -> 398 us (0.89)
  local copies, waits for them, and re-layouts: 102 us -> 56.5 us
  other arithmetic: 19.6 us -> 1.49 us
  waiting for transfers between devices: 234 us -> 251 us
    reduce_scatter x1 -> x0, waiting for transfers between devices: 78.3 us -> none  [local(): lax.psum_scatter(on_chip, 'dpo', scatter_dimension=0, tiled=True)]
    unnamed x4 -> x7, waiting for transfers between devices: 0.07 us -> 67.5 us
    slice x2 -> x4, local copies, waits for them, and re-layouts: 65.4 us -> 0.84 us  [the longest x2 0.59 us: local(): g_blocks = gather(recv[1])]
    all_gather x2 -> x4, waiting for transfers between devices: 132 us -> 169 us  [the longest x2 124 us: gather(): half = lax.all_gather(part, 'dpo', axis=0, tiled=True)]
    all_gather x0 -> x4, local copies, waits for them, and re-layouts: none -> 30.6 us  [the longest x2 19.3 us: gather(): return lax.all_gather(half, 'core', axis=0, tiled=True)]
    unnamed x2 -> x1, other arithmetic: 18.1 us -> 0.01 us
    another operation x3 -> x1, local copies, waits for them, and re-layouts: 14.6 us -> 0.01 us  [the longest x1 7.32 us: local(): grads_in = full[:, 1].reshape(n_rows, d_all)]
    reduce_scatter x1, waiting for transfers between devices: 23.7 us -> 15 us  [local(): on_chip = lax.psum_scatter(blocks, 'core', scatter_dimension=0, tiled=True)]
  transfers between devices with their start and end apart: 5 -> 7, of which waited for: 4 -> 6; matrix products, arithmetic and copies ran while one was open for 6% -> 19% of each run, Pallas kernels for 0% -> 0%
where the time goes in v2:
time: 398 us; the launch traced here: 396 us
  waiting for transfers between devices  251 us (63%)
  local copies, waits for them, and re-layouts  56.5 us (14%)
  matrix products  35.7 us (9%)
  blocking collectives  31.2 us (8%)
  between operations  14.3 us (4%)
  starting transfers between devices  5.46 us (1%)
    all_gather x2, waiting for transfers between devices, gather(): half = lax.all_gather(part, 'dpo', axis=0, tiled=True)  124 us
    unnamed x7, waiting for transfers between devices  67.5 us
    all_gather x2, waiting for transfers between devices, gather(): return lax.all_gather(half, 'core', axis=0, tiled=True)  44.7 us
    all_gather x2, local copies, waits for them, and re-layouts, gather(): return lax.all_gather(half, 'core', axis=0, tiled=True)  19.3 us
    psum x1, blocking collectives, local(): d_route = lax.psum(partial_dots, 'expert')  18 us
    reduce_scatter x1, waiting for transfers between devices, local(): on_chip = lax.psum_scatter(blocks, 'core', scatter_dimension=0, tiled=True)  15 us
    all_to_all x1, blocking collectives, local(): lax.all_to_all(sent, 'expert', split_axis=1, concat_axis=3, tiled=True)  13.2 us
    all_gather x2, local copies, waits for them, and re-layouts, gather(): half = lax.all_gather(part, 'dpo', axis=0, tiled=True)  11.3 us
  transfers between devices with their start and end apart: 7, of which 6 were waited for; matrix products, arithmetic and copies ran while one was open for 19% of the time, Pallas kernels for 0%

profile of v2, /device:TPU:2, one launch (start us, length us, event | category | flops | bytes accessed | tf_op | source)
XLA Modules:
  0.0 396.1 jit_solution(3237596640254596057)
XLA Ops:
  7.2 0.9 copy.50
  8.1 0.1 eq.60
  8.3 0.1 eq.56
  8.4 0.8 slice_bitcast_fusion.2
  9.2 0.6 reduce-window.6
  9.7 0.2 slice_reduce_fusion
  10.0 0.1 fusion.29
  10.1 0.1 reshape.61
  10.3 0.7 multiply_add_fusion
  11.0 1.1 convolution_convert_fusion.5
  12.1 0.1 reshape.62
  12.2 1.3 convolution_convert_fusion.4
  13.5 0.1 reshape.63
  13.6 0.4 copy.53
  14.1 13.2 %all_to_all.24 = bf16[2,8,33,384]{3,0,2,1:T(2,128)(2,1)S(1)} all-to-all(bf16[2,8,33,384]{3,0,2,1:T(2,128)(2,1)S(1)} %copy.53), channel_id=1, replica_groups=mesh['dpo'=16,'core'=2,'expert'=8] {'expert'}, dimensions={1} | all-to-all | bytes 811008 | tf_op jit(solution)/shard_map/all_to_all | solution.py:41
  27.3 0.6 fusion.35
  27.9 0.8 squeeze.15
  28.8 76.5 %all-gather.5.cloned.1.call-done = bf16[16,33,3072]{2,1,0:T(8,128)(2,1)} async-done(((bf16[1,33,3072]{2,1,0:T(8,128)(2,1)}), bf16[16,33,3072]{2,1,0:T(8,128)(2,1)}) %all-gather.5.cloned.1.call-update) | async-done | bytes 3244048 | tf_op jit(solution)/shard_map/all_gather | solution.py:44
  105.3 5.7 %copy.55 = bf16[16,33,3072]{2,0,1:T(8,128)(2,1)} copy(bf16[16,33,3072]{2,1,0:T(8,128)(2,1)} %all-gather.5.cloned.1.call-done) | data formatting | bytes 6488064 | tf_op jit(solution)/shard_map/all_gather | solution.py:44
  111.1 0.8 squeeze.19
  111.9 0.2 reduce-scatter.5.cloned.1.call-start
  112.1 19.4 %all-gather.7.cloned.1.call-done = bf16[32,33,3072]{2,0,1:T(8,128)(2,1)} async-done(((bf16[16,33,3072]{2,0,1:T(8,128)(2,1)}), bf16[32,33,3072]{2,0,1:T(8,128)(2,1)}) %all-gather.7.cloned.1.call-update) | async-done | bytes 6488080 | tf_op jit(solution)/shard_map/all_gather | solution.py:45
  131.5 9.6 %copy.56 = bf16[32,33,3072]{2,1,0:T(8,128)(2,1)} copy(bf16[32,33,3072]{2,0,1:T(8,128)(2,1)} %all-gather.7.cloned.1.call-done) | data formatting | bytes 12976128 | tf_op jit(solution)/shard_map/all_gather | solution.py:45
  141.2 7.2 %reshape.64 = bf16[1056,3072]{1,0:T(8,128)(2,1)} reshape(bf16[32,33,3072]{2,1,0:T(8,128)(2,1)} %copy.56) | data formatting | bytes 12976128 | tf_op jit(solution)/shard_map/reshape | solution.py:52
  148.3 5.4 %fusion.8 = f32[1056,256]{1,0:T(8,128)S(1)} fusion(bf16[1056,3072]{1,0:T(8,128)(2,1)} %reshape.64, bf16[1,3072,256]{2,1,0:T(8,128)(2,1)} %param.11), kind=kOutput, calls=%fused_computation.12 | convolution fusion | flops 1660944384 | bytes 9142272 | tf_op jit(solution)/shard_map/dot_general | solution.py:58
  153.7 0.3 copy-done.2
  154.0 2.9 multiply_convert_fusion.2
  156.9 1.9 convolution_convert_fusion
  158.8 4.3 %copy.61 = bf16[132,8,8,384]{3,2,1,0:T(8,128)(2,1)} copy(bf16[132,8,8,384]{3,1,2,0:T(8,128)(2,1)S(1)} %bitcast.65) | data formatting | bytes 12976128
  163.2 47.8 %all-gather.9.cloned.1.call-done = bf16[16,33,3072]{2,1,0:T(8,128)(2,1)} async-done(((bf16[1,33,3072]{2,1,0:T(8,128)(2,1)}), bf16[16,33,3072]{2,1,0:T(8,128)(2,1)}) %all-gather.9.cloned.1.call-update) | async-done | bytes 3244048 | tf_op jit(solution)/shard_map/all_gather | solution.py:44
  211.0 5.7 %copy.59 = bf16[16,33,3072]{2,0,1:T(8,128)(2,1)} copy(bf16[16,33,3072]{2,1,0:T(8,128)(2,1)} %all-gather.9.cloned.1.call-done) | data formatting | bytes 6488064 | tf_op jit(solution)/shard_map/all_gather | solution.py:44
  216.7 0.3 reduce-scatter.7.cloned.1.call-start
  216.9 15.0 %reduce-scatter.5.cloned.1.call-done = bf16[16,8,33,384]{3,1,2,0:T(8,128)(2,1)} async-done(((bf16[32,8,33,384]{3,1,2,0:T(8,128)(2,1)}), bf16[16,8,33,384]{3,1,2,0:T(8,128)(2,1)}) %reduce-scatter.5.cloned.1.call-update) | async-done | bytes 3244048 | tf_op jit(solution)/shard_map/reduce_scatter | solution.py:80
  231.9 25.3 %all-gather.11.cloned.1.call-done = bf16[32,33,3072]{2,0,1:T(8,128)(2,1)} async-done(((bf16[16,33,3072]{2,0,1:T(8,128)(2,1)}), bf16[32,33,3072]{2,0,1:T(8,128)(2,1)}) %all-gather.11.cloned.1.call-update) | async-done | bytes 6488080 | tf_op jit(solution)/shard_map/all_gather | solution.py:45
  257.3 9.7 %copy.60 = bf16[32,33,3072]{2,1,0:T(8,128)(2,1)} copy(bf16[32,33,3072]{2,0,1:T(8,128)(2,1)} %all-gather.11.cloned.1.call-done) | data formatting | bytes 12976128 | tf_op jit(solution)/shard_map/all_gather | solution.py:45
  266.9 7.1 %reshape.67 = bf16[1056,3072]{1,0:T(8,128)(2,1)} reshape(bf16[32,33,3072]{2,1,0:T(8,128)(2,1)} %copy.60) | data formatting | bytes 12976128 | tf_op jit(solution)/shard_map/reshape | solution.py:53
  274.1 4.9 %fusion.3 = f32[1056,256]{1,0:T(8,128)S(1)} fusion(bf16[1056,3072]{1,0:T(8,128)(2,1)} %reshape.67, bf16[1,256,3072]{2,1,0:T(8,128)(2,1)S(1)} %copy-done), kind=kOutput, calls=%fused_computation.7 | convolution fusion | flops 1660944384 | bytes 9142272 | tf_op jit(solution)/shard_map/rd,fd->rf/dot_general | solution.py:64
  279.0 6.6 %fusion.1 = bf16[1,3072,256]{2,1,0:T(8,128)(2,1)} fusion(bf16[1056,3072]{1,0:T(8,128)(2,1)} %reshape.64, f32[1056,256]{1,0:T(8,128)S(1)} %fusion.3, f32[1056,256]{1,0:T(8,128)S(1)} %fusion.8), kind=kOutput, calls=%fused_computation.5 | convolution fusion | flops 1663352832 | bytes 10223616 | tf_op jit(solution)/shard_map/rd,rf->df/dot_general | solution.py:75
  285.6 3.6 fusion
  289.2 67.4 %reduce-scatter.7.cloned.1.call-done = bf16[1,8,33,384]{3,1,2,0:T(8,128)(2,1)} async-done(((bf16[16,8,33,384]{3,1,2,0:T(8,128)(2,1)}), bf16[1,8,33,384]{3,1,2,0:T(8,128)(2,1)}) %reduce-scatter.7.cloned.1.call-update) | async-done | bytes 202768
  356.6 1.7 copy.57
  358.3 4.8 %all-to-all-start.1 = ((bf16[1,8,33,384]{3,2,0,1:T(8,128)(2,1)}), bf16[1,8,33,384]{3,2,0,1:T(8,128)(2,1)S(1)}, u32[]{:S(2)}, u32[]{:S(2)}) async-start(bf16[1,8,33,384]{3,2,0,1:T(8,128)(2,1)} %copy.57), calls=%async_computation.2 | async-start | bytes 491520 | tf_op jit(solution)/shard_map/all_to_all | solution.py:82
  363.1 6.3 %fusion.2 = bf16[1,256,3072]{2,1,0:T(8,128)(2,1)} fusion(bf16[1056,256]{1,0:T(8,128)(2,1)S(1)} %get-tuple-element.11, bf16[1056,3072]{1,0:T(8,128)(2,1)} %reshape.67), kind=kOutput, calls=%fused_computation.6 | convolution fusion | flops 1661730816 | bytes 8601600 | tf_op jit(solution)/shard_map/rf,rd->fd/dot_general | solution.py:65
  369.3 0.1 reshape.66
  369.4 0.4 fusion.11
  369.8 0.4 fusion.10
  370.2 1.1 convolution_convert_fusion.6
  371.3 18.0 %psum.7 = f32[128,2]{0,1:T(2,128)} all-reduce(f32[128,2]{0,1:T(2,128)S(1)} %pad_maximum_fusion.1), channel_id=1, replica_groups=mesh['dpo'=16,'core'=2,'expert'=8] {'expert'}, use_global_device_ids=true, to_apply=%region_7.8 | all-reduce | flops 256 | bytes 2048 | tf_op jit(solution)/shard_map/psum | solution.py:93
  (34 shorter events, 0.6 us)
Async XLA Ops:
  7.2 149.8 %copy-start = (bf16[1,256,3072]{2,1,0:T(8,128)(2,1)S(1)}, bf16[1,256,3072]{2,1,0:T(8,128)(2,1)}, u32[]{:S(2)}) copy-start(bf16[1,256,3072]{2,1,0:T(8,128)(2,1)} %param.13) | copy-start | bytes 4718596
  7.2 98.1 %all-gather.5.cloned.1.call-start = ((), (), s32[]{:S(2)}) async-start(), calls=%async_computation.4 | async-start | bytes 4177920 | tf_op jit(solution)/shard_map/all_gather | solution.py:44
  28.8 102.8 %all-gather.7.cloned.1.call-start = ((), (), s32[]{:S(2)}) async-start(), calls=%async_computation.5 | async-start | bytes 9732096 | tf_op jit(solution)/shard_map/all_gather | solution.py:45
  111.0 100.0 %all-gather.9.cloned.1.call-start = ((), (), s32[]{:S(2)}) async-start(), calls=%async_computation.7 | async-start | bytes 4177920 | tf_op jit(solution)/shard_map/all_gather | solution.py:44
  111.9 120.0 %reduce-scatter.5.cloned.1.call-start = ((), (), s32[]{:S(2)}) async-start(), calls=%async_computation.6 | async-start | bytes 9732096 | tf_op jit(solution)/shard_map/reduce_scatter | solution.py:80
  148.3 5.4 %copy-start.1 = (bf16[1056,3072]{1,0:T(8,128)(2,1)S(1)}, bf16[1056,3072]{1,0:T(8,128)(2,1)}, u32[]{:S(2)}) copy-start(bf16[1056,3072]{1,0:T(8,128)(2,1)} %reshape.64) | copy-start | bytes 19464196
  148.3 5.7 %copy-start.2 = (bf16[1,3072,256]{2,1,0:T(8,128)(2,1)S(1)}, bf16[1,3072,256]{2,1,0:T(8,128)(2,1)}, u32[]{:S(2)}) copy-start(bf16[1,3072,256]{2,1,0:T(8,128)(2,1)} %param.12) | copy-start | bytes 4718596
  163.2 94.1 %all-gather.11.cloned.1.call-start = ((), (), s32[]{:S(2)}) async-start(), calls=%async_computation.8 | async-start | bytes 9732096 | tf_op jit(solution)/shard_map/all_gather | solution.py:45
  216.7 139.9 %reduce-scatter.7.cloned.1.call-start = ((), (), s32[]{:S(2)}) async-start(), calls=%async_computation.9 | async-start | bytes 3446784
  274.1 11.5 %slice-start = ((s8[6488064]{0:T(1024)(128)(4,1)}), s8[4194304]{0:T(1024)(128)(4,1)S(1)}, s32[]{:S(2)}) async-start(s8[6488064]{0:T(1024)(128)(4,1)} %bitcast.67), calls=%async_computation.10 | async-start | bytes 8388608
  279.0 6.6 %slice-start.1 = ((s8[6488064]{0:T(1024)(128)(4,1)}), s8[2293760]{0:T(1024)(128)(4,1)S(1)}, s32[]{:S(2)}) async-start(s8[6488064]{0:T(1024)(128)(4,1)} %bitcast.67), calls=%async_computation.11 | async-start | bytes 4587520
  279.0 6.6 %copy-start.4 = (f32[1056,256]{1,0:T(8,128)S(1)}, f32[1056,256]{1,0:T(8,128)}, u32[]{:S(2)}) copy-start(f32[1056,256]{1,0:T(8,128)} %get-tuple-element.12) | copy-start | bytes 3244036
  358.3 11.1 %all-to-all-start.1 = ((bf16[1,8,33,384]{3,2,0,1:T(8,128)(2,1)}), bf16[1,8,33,384]{3,2,0,1:T(8,128)(2,1)S(1)}, u32[]{:S(2)}, u32[]{:S(2)}) async-start(bf16[1,8,33,384]{3,2,0,1:T(8,128)(2,1)} %copy.57), calls=%async_computation.2 | async-start | bytes 491520 | tf_op jit(solution)/shard_map/all_to_all | solution.py:82
  363.1 6.3 %copy-start.3 = (bf16[128,384]{1,0:T(8,128)(2,1)S(1)}, bf16[128,384]{1,0:T(8,128)(2,1)}, u32[]{:S(2)}) copy-start(bf16[128,384]{1,0:T(8,128)(2,1)} %param.8) | copy-start | bytes 294916
Sparse Core Ops, SparseCore 0:
  28.9 76.3 all-gather.4
  111.1 20.3 all-gather.6
  134.6 76.3 all-gather.8
  213.4 18.4 reduce-scatter.4
  233.6 23.6 all-gather.10
  260.8 95.7 reduce-scatter.6

commit v3 on v2

--- a/solution.py
+++ b/solution.py
@@ -40,9 +40,11 @@
     sent = jnp.concatenate([sent_tokens, sent_grads], axis=0)
     recv = lax.all_to_all(sent, "expert", split_axis=1, concat_axis=3, tiled=True)
 
+    n_dp = lax.axis_size(DP)
+
     def gather(part):
-        half = lax.all_gather(part, "dpo", axis=0, tiled=True)
-        return lax.all_gather(half, "core", axis=0, tiled=True)
+        spread = jnp.broadcast_to(part, (n_dp,) + part.shape[1:])
+        return lax.all_to_all(spread, DP, split_axis=0, concat_axis=0, tiled=True)
 
     x_blocks = gather(recv[0])
     g_blocks = gather(recv[1])
@@ -77,9 +79,9 @@
     )
 
     blocks = partial_out.reshape(n_blk, capacity, experts, d_all // experts).transpose(0, 2, 1, 3)
-    on_chip = lax.psum_scatter(blocks, "core", scatter_dimension=0, tiled=True)
-    summed_out = lax.psum_scatter(on_chip, "dpo", scatter_dimension=0, tiled=True)
-    returned_out = lax.all_to_all(summed_out, "expert", split_axis=1, concat_axis=0, tiled=True)
+    slabs = lax.all_to_all(blocks, DP, split_axis=0, concat_axis=0, tiled=True)
+    summed_out = jnp.sum(slabs.astype(jnp.float32), axis=0).astype(jnp.bfloat16)
+    returned_out = lax.all_to_all(summed_out, "expert", split_axis=0, concat_axis=0, tiled=True)
     flat_out = returned_out.reshape(experts * capacity, -1).astype(jnp.float32)
     combined = jnp.dot(weighted.T, flat_out, precision=highest).astype(jnp.bfloat16)
     grads32 = out_grad.astype(jnp.float32)

time: 398 us -> 587 us (1.47)
  waiting for transfers between devices: 251 us -> 453 us
  local copies, waits for them, and re-layouts: 56.5 us -> 31.5 us
  starting transfers between devices: 5.46 us -> 28.3 us
  between operations: 14.3 us -> 0.87 us
    all_to_all x1 -> x4, waiting for transfers between devices: 0.01 us -> 453 us  [the longest x2 330 us: gather(): return lax.all_to_all(spread, DP, split_axis=0, concat_axis=0, tiled=True)]
    all_gather x4 -> x0, waiting for transfers between devices: 169 us -> none  [the longest x2 124 us: gather(): half = lax.all_gather(part, 'dpo', axis=0, tiled=True)]
    unnamed x7 -> x0, waiting for transfers between devices: 67.5 us -> none
    all_gather x4 -> x0, local copies, waits for them, and re-layouts: 30.6 us -> none  [the longest x2 19.3 us: gather(): return lax.all_gather(half, 'core', axis=0, tiled=True)]
    all_to_all x1 -> x4, starting transfers between devices: 4.81 us -> 28.3 us  [the longest x2 15.6 us: gather(): return lax.all_to_all(spread, DP, split_axis=0, concat_axis=0, tiled=True)]
    reduce_scatter x1 -> x0, waiting for transfers between devices: 15 us -> none  [local(): on_chip = lax.psum_scatter(blocks, 'core', scatter_dimension=0, tiled=True)]
    broadcast_in_dim x0 -> x2, local copies, waits for them, and re-layouts: none -> 8.18 us  [gather(): spread = jnp.broadcast_to(part, (n_dp,) + part.shape[1:])]
  transfers between devices with their start and end apart: 7 -> 4, of which waited for: 6 -> 3; matrix products, arithmetic and copies ran while one was open for 19% -> 9% of each run, Pallas kernels for 0% -> 0%
where the time goes in v3:
time: 587 us; the launch traced here: 586 us
  waiting for transfers between devices  453 us (77%)
  matrix products  35.5 us (6%)
  local copies, waits for them, and re-layouts  31.5 us (5%)
  blocking collectives  31.3 us (5%)
  starting transfers between devices  28.3 us (5%)
    all_to_all x2, waiting for transfers between devices, gather(): return lax.all_to_all(spread, DP, split_axis=0, concat_axis=0, tiled=True)  330 us
    all_to_all x1, waiting for transfers between devices, local(): slabs = lax.all_to_all(blocks, DP, split_axis=0, concat_axis=0, tiled=True)  123 us
    psum x1, blocking collectives, local(): d_route = lax.psum(partial_dots, 'expert')  18 us
    all_to_all x2, starting transfers between devices, gather(): return lax.all_to_all(spread, DP, split_axis=0, concat_axis=0, tiled=True)  15.6 us
    all_to_all x1, blocking collectives, local(): lax.all_to_all(sent, 'expert', split_axis=1, concat_axis=3, tiled=True)  13.2 us
  transfers between devices with their start and end apart: 4, of which 3 were waited for; matrix products, arithmetic and copies ran while one was open for 9% of the time, Pallas kernels for 0%

profile of v3, /device:TPU:2, one launch (start us, length us, event | category | flops | bytes accessed | tf_op | source)
XLA Modules:
  0.0 586.0 jit_solution(13985286699835595360)
XLA Ops:
  0.6 0.0 copy-start
  0.6 0.9 copy.40
  1.6 0.1 eq.60
  1.7 0.1 eq.56
  1.8 0.8 slice_bitcast_fusion.2
  2.6 0.6 reduce-window.6
  3.2 0.2 slice_reduce_fusion
  3.4 0.1 fusion.29
  3.5 0.1 reshape.59
  3.7 0.1 copy.42
  3.7 0.7 multiply_add_fusion
  4.4 1.1 convolution_convert_fusion.5
  5.6 0.1 reshape.60
  5.6 1.3 convolution_convert_fusion.4
  6.9 0.1 reshape.61
  7.0 0.1 pad_maximum_fusion
  7.1 0.4 copy.43
  7.5 13.2 %all_to_all.35 = bf16[2,8,33,384]{3,0,2,1:T(2,128)(2,1)S(1)} all-to-all(bf16[2,8,33,384]{3,0,2,1:T(2,128)(2,1)S(1)} %copy.43), channel_id=1, replica_groups=mesh['dpo'=16,'core'=2,'expert'=8] {'expert'}, dimensions={1} | all-to-all | bytes 811008 | tf_op jit(solution)/shard_map/all_to_all | solution.py:41
  20.8 0.6 fusion.35
  21.3 0.1 copy_bitcast_fusion
  21.5 4.1 broadcast_in_dim.26
  25.5 10.7 %all-to-all-start.1 = ((bf16[32,33,3072]{2,1,0:T(8,128)(2,1)}), bf16[32,33,3072]{2,1,0:T(8,128)(2,1)}, u32[]{:S(2)}, u32[]{:S(2)}) async-start(bf16[32,33,3072]{2,1,0:T(8,128)(2,1)} %broadcast_in_dim.26), calls=%async_computation.1 | async-start | bytes 15728640 | tf_op jit(solution)/shard_map/all_to_all | solution.py:47
  36.3 176.3 %all-to-all-done.1 = bf16[32,33,3072]{2,1,0:T(8,128)(2,1)} async-done(((bf16[32,33,3072]{2,1,0:T(8,128)(2,1)}), bf16[32,33,3072]{2,1,0:T(8,128)(2,1)}, u32[]{:S(2)}, u32[]{:S(2)}) %all-to-all-start.1) | async-done | bytes 6488096 | tf_op jit(solution)/shard_map/all_to_all | solution.py:47
  212.7 4.1 broadcast_in_dim.28
  216.8 4.9 all-to-all-start.4
  221.7 7.1 %reshape.62 = bf16[1056,3072]{1,0:T(8,128)(2,1)} reshape(bf16[32,33,3072]{2,1,0:T(8,128)(2,1)} %all-to-all-done.1) | data formatting | bytes 12976128 | tf_op jit(solution)/shard_map/reshape | solution.py:54
  228.8 5.3 fusion.8
  234.1 0.3 copy-done.2
  234.4 2.9 multiply_convert_fusion.2
  237.3 1.9 convolution_convert_fusion
  239.2 4.3 copy.48
  243.5 153.4 %all-to-all-done.4 = bf16[32,33,3072]{2,1,0:T(8,128)(2,1)} async-done(((bf16[32,33,3072]{2,1,0:T(8,128)(2,1)}), bf16[32,33,3072]{2,1,0:T(8,128)(2,1)}, u32[]{:S(2)}, u32[]{:S(2)}) %all-to-all-start.4) | async-done | bytes 6488096 | tf_op jit(solution)/shard_map/all_to_all | solution.py:47
  396.8 5.1 all-to-all-start.2
  402.0 7.1 %reshape.65 = bf16[1056,3072]{1,0:T(8,128)(2,1)} reshape(bf16[32,33,3072]{2,1,0:T(8,128)(2,1)} %all-to-all-done.4) | data formatting | bytes 12976128 | tf_op jit(solution)/shard_map/reshape | solution.py:55
  409.1 4.9 fusion.3
  414.0 0.0 copy-start.4
  414.0 6.5 %fusion.1 = bf16[1,3072,256]{2,1,0:T(8,128)(2,1)} fusion(bf16[1056,3072]{1,0:T(8,128)(2,1)} %reshape.62, f32[1056,256]{1,0:T(8,128)S(1)} %fusion.3, f32[1056,256]{1,0:T(8,128)S(1)} %fusion.8), kind=kOutput, calls=%fused_computation.5 | convolution fusion | flops 1663352832 | bytes 10223616 | tf_op jit(solution)/shard_map/rd,rf->df/dot_general | solution.py:77
  420.5 3.6 fusion
  424.1 123.4 %all-to-all-done.2 = bf16[32,8,33,384]{3,1,2,0:T(8,128)(2,1)} async-done(((bf16[32,8,33,384]{3,1,2,0:T(8,128)(2,1)}), bf16[32,8,33,384]{3,1,2,0:T(8,128)(2,1)}, u32[]{:S(2)}, u32[]{:S(2)}) %all-to-all-start.2) | async-done | bytes 6488096 | tf_op jit(solution)/shard_map/all_to_all | solution.py:82
  547.6 3.9 reduce_sum.40
  551.5 0.7 copy.45
  552.2 7.6 %all-to-all-start.3 = ((bf16[8,33,384]{2,1,0:T(8,128)(2,1)}), bf16[8,33,384]{2,1,0:T(8,128)(2,1)S(1)}, u32[]{:S(2)}, u32[]{:S(2)}) async-start(bf16[8,33,384]{2,1,0:T(8,128)(2,1)} %copy.45), calls=%async_computation.3 | async-start | bytes 491520 | tf_op jit(solution)/shard_map/all_to_all | solution.py:84
  559.8 6.3 %fusion.2 = bf16[1,256,3072]{2,1,0:T(8,128)(2,1)} fusion(bf16[1056,256]{1,0:T(8,128)(2,1)S(1)} %get-tuple-element.11, bf16[1056,3072]{1,0:T(8,128)(2,1)} %reshape.65), kind=kOutput, calls=%fused_computation.6 | convolution fusion | flops 1661730816 | bytes 8601600 | tf_op jit(solution)/shard_map/rf,rd->fd/dot_general | solution.py:67
  566.1 0.1 reshape.64
  566.1 0.4 fusion.11
  566.5 0.4 fusion.10
  566.9 1.1 convolution_convert_fusion.6
  568.0 18.0 %psum.7 = f32[128,2]{0,1:T(2,128)} all-reduce(f32[128,2]{0,1:T(2,128)S(1)} %pad_maximum_fusion.1), channel_id=1, replica_groups=mesh['dpo'=16,'core'=2,'expert'=8] {'expert'}, use_global_device_ids=true, to_apply=%region_6.7 | all-reduce | flops 256 | bytes 2048 | tf_op jit(solution)/shard_map/psum | solution.py:95
  (22 shorter events, 0.2 us)
Async XLA Ops:
  0.6 236.7 %copy-start = (bf16[1,256,3072]{2,1,0:T(8,128)(2,1)S(1)}, bf16[1,256,3072]{2,1,0:T(8,128)(2,1)}, u32[]{:S(2)}) copy-start(bf16[1,256,3072]{2,1,0:T(8,128)(2,1)} %param.13) | copy-start | bytes 4718596
  25.5 187.1 %all-to-all-start.1 = ((bf16[32,33,3072]{2,1,0:T(8,128)(2,1)}), bf16[32,33,3072]{2,1,0:T(8,128)(2,1)}, u32[]{:S(2)}, u32[]{:S(2)}) async-start(bf16[32,33,3072]{2,1,0:T(8,128)(2,1)} %broadcast_in_dim.26), calls=%async_computation.1 | async-start | bytes 15728640 | tf_op jit(solution)/shard_map/all_to_all | solution.py:47
  216.8 180.1 %all-to-all-start.4 = ((bf16[32,33,3072]{2,1,0:T(8,128)(2,1)}), bf16[32,33,3072]{2,1,0:T(8,128)(2,1)}, u32[]{:S(2)}, u32[]{:S(2)}) async-start(bf16[32,33,3072]{2,1,0:T(8,128)(2,1)} %broadcast_in_dim.28), calls=%async_computation.4 | async-start | bytes 15728640 | tf_op jit(solution)/shard_map/all_to_all | solution.py:47
  228.8 5.3 copy-start.1
  228.8 5.6 copy-start.2
  396.8 150.7 %all-to-all-start.2 = ((bf16[32,8,33,384]{3,1,2,0:T(8,128)(2,1)}), bf16[32,8,33,384]{3,1,2,0:T(8,128)(2,1)}, u32[]{:S(2)}, u32[]{:S(2)}) async-start(bf16[32,8,33,384]{3,1,2,0:T(8,128)(2,1)} %bitcast.69), calls=%async_computation.2 | async-start | bytes 12976128 | tf_op jit(solution)/shard_map/all_to_all | solution.py:82
  409.1 11.4 %slice-start = ((s8[6488064]{0:T(1024)(128)(4,1)}), s8[4194304]{0:T(1024)(128)(4,1)S(1)}, s32[]{:S(2)}) async-start(s8[6488064]{0:T(1024)(128)(4,1)} %bitcast.70), calls=%async_computation.5 | async-start | bytes 8388608
  414.0 6.5 %slice-start.1 = ((s8[6488064]{0:T(1024)(128)(4,1)}), s8[2293760]{0:T(1024)(128)(4,1)S(1)}, s32[]{:S(2)}) async-start(s8[6488064]{0:T(1024)(128)(4,1)} %bitcast.70), calls=%async_computation.6 | async-start | bytes 4587520
  414.0 6.5 %copy-start.4 = (f32[1056,256]{1,0:T(8,128)S(1)}, f32[1056,256]{1,0:T(8,128)}, u32[]{:S(2)}) copy-start(f32[1056,256]{1,0:T(8,128)} %get-tuple-element.12) | copy-start | bytes 3244036
  552.2 13.8 %all-to-all-start.3 = ((bf16[8,33,384]{2,1,0:T(8,128)(2,1)}), bf16[8,33,384]{2,1,0:T(8,128)(2,1)S(1)}, u32[]{:S(2)}, u32[]{:S(2)}) async-start(bf16[8,33,384]{2,1,0:T(8,128)(2,1)} %copy.45), calls=%async_computation.3 | async-start | bytes 491520 | tf_op jit(solution)/shard_map/all_to_all | solution.py:84
  559.8 6.3 %copy-start.3 = (bf16[128,384]{1,0:T(8,128)(2,1)S(1)}, bf16[128,384]{1,0:T(8,128)(2,1)}, u32[]{:S(2)}) copy-start(bf16[128,384]{1,0:T(8,128)(2,1)} %param.8) | copy-start | bytes 294916

commit v4 on v2

--- a/solution.py
+++ b/solution.py
@@ -40,17 +40,13 @@
     sent = jnp.concatenate([sent_tokens, sent_grads], axis=0)
     recv = lax.all_to_all(sent, "expert", split_axis=1, concat_axis=3, tiled=True)
 
-    def gather(part):
-        half = lax.all_gather(part, "dpo", axis=0, tiled=True)
-        return lax.all_gather(half, "core", axis=0, tiled=True)
-
-    x_blocks = gather(recv[0])
-    g_blocks = gather(recv[1])
-    n_blk = x_blocks.shape[0]
-    d_all = x_blocks.shape[2]
+    both = jnp.concatenate([recv[0], recv[1]], axis=-1)
+    blocks_all = lax.all_gather(both, DP, axis=0, tiled=True)
+    n_blk = blocks_all.shape[0]
+    d_all = recv.shape[-1]
     n_rows = n_blk * capacity
-    gathered = x_blocks.reshape(n_rows, d_all)
-    grads_in = g_blocks.reshape(n_rows, d_all)
+    gathered = blocks_all[:, :, :d_all].reshape(n_rows, d_all)
+    grads_in = blocks_all[:, :, d_all:].reshape(n_rows, d_all)
     gate_slab = w_gate[0]
     up_slab = w_up[0]
     down_slab = w_down[0]
@@ -77,8 +73,7 @@
     )
 
     blocks = partial_out.reshape(n_blk, capacity, experts, d_all // experts).transpose(0, 2, 1, 3)
-    on_chip = lax.psum_scatter(blocks, "core", scatter_dimension=0, tiled=True)
-    summed_out = lax.psum_scatter(on_chip, "dpo", scatter_dimension=0, tiled=True)
+    summed_out = lax.psum_scatter(blocks, DP, scatter_dimension=0, tiled=True)
     returned_out = lax.all_to_all(summed_out, "expert", split_axis=1, concat_axis=0, tiled=True)
     flat_out = returned_out.reshape(experts * capacity, -1).astype(jnp.float32)
     combined = jnp.dot(weighted.T, flat_out, precision=highest).astype(jnp.bfloat16)

time: 398 us -> 323 us (0.81)
  waiting for transfers between devices: 251 us -> 198 us
  local copies, waits for them, and re-layouts: 56.5 us -> 35.4 us
    all_gather x4 -> x1, waiting for transfers between devices: 169 us -> 106 us  [local(): blocks_all = lax.all_gather(both, DP, axis=0, tiled=True)]
    all_gather x4 -> x0, local copies, waits for them, and re-layouts: 30.6 us -> none  [the longest x2 19.3 us: gather(): return lax.all_gather(half, 'core', axis=0, tiled=True)]
    unnamed x7 -> x3, waiting for transfers between devices: 67.5 us -> 92.1 us
    reduce_scatter x1 -> x0, waiting for transfers between devices: 15 us -> none  [local(): on_chip = lax.psum_scatter(blocks, 'core', scatter_dimension=0, tiled=True)]
    slice x4 -> x5, local copies, waits for them, and re-layouts: 0.84 us -> 11.8 us  [the longest x1 11 us: local(): grads_in = blocks_all[:, :, d_all:].reshape(n_rows, d_all)]
  transfers between devices with their start and end apart: 7 -> 3, of which waited for: 6 -> 2; matrix products, arithmetic and copies ran while one was open for 19% -> 9% of each run, Pallas kernels for 0% -> 0%
where the time goes in v4:
time: 323 us; the launch traced here: 322 us
  waiting for transfers between devices  198 us (61%)
  matrix products  35.6 us (11%)
  local copies, waits for them, and re-layouts  35.4 us (11%)
  blocking collectives  31.2 us (10%)
  between operations  14.2 us (4%)
  starting transfers between devices  4.79 us (1%)
    all_gather x1, waiting for transfers between devices, local(): blocks_all = lax.all_gather(both, DP, axis=0, tiled=True)  106 us
    unnamed x3, waiting for transfers between devices  92.1 us
    psum x1, blocking collectives, local(): d_route = lax.psum(partial_dots, 'expert')  18 us
    all_to_all x1, blocking collectives, local(): lax.all_to_all(sent, 'expert', split_axis=1, concat_axis=3, tiled=True)  13.2 us
    slice x1, local copies, waits for them, and re-layouts, local(): grads_in = blocks_all[:, :, d_all:].reshape(n_rows, d_all)  11 us
    reshape x1, local copies, waits for them, and re-layouts, local(): grads_in = blocks_all[:, :, d_all:].reshape(n_rows, d_all)  7.13 us
    reshape x1, local copies, waits for them, and re-layouts, local(): gathered = blocks_all[:, :, :d_all].reshape(n_rows, d_all)  7.11 us
    dot_general x1, matrix products, local(): jnp.einsum('rd,rf->df', gathered, d_up_act, preferred_element_type=jnp.fl...  6.54 us
  transfers between devices with their start and end apart: 3, of which 2 were waited for; matrix products, arithmetic and copies ran while one was open for 9% of the time, Pallas kernels for 0%

profile of v4, /device:TPU:2, one launch (start us, length us, event | category | flops | bytes accessed | tf_op | source)
XLA Modules:
  0.0 321.7 jit_solution(757043136803514270)
XLA Ops:
  7.2 0.0 copy-start
  7.2 0.0 all-gather.2.cloned.1.call-start
  7.2 0.9 copy.42
  8.1 0.1 eq.60
  8.3 0.1 eq.56
  8.4 0.8 slice_bitcast_fusion.2
  9.2 0.6 reduce-window.6
  9.7 0.2 slice_reduce_fusion
  10.0 0.1 fusion.29
  10.1 0.1 reshape.61
  10.2 0.1 copy.44
  10.3 0.7 multiply_add_fusion
  11.0 1.1 convolution_convert_fusion.5
  12.1 0.1 reshape.62
  12.2 1.3 convolution_convert_fusion.4
  13.5 0.1 reshape.63
  13.6 0.1 pad_maximum_fusion
  13.6 0.4 copy.45
  14.1 13.2 %all_to_all.24 = bf16[2,8,33,384]{3,0,2,1:T(2,128)(2,1)S(1)} all-to-all(bf16[2,8,33,384]{3,0,2,1:T(2,128)(2,1)S(1)} %copy.45), channel_id=1, replica_groups=mesh['dpo'=16,'core'=2,'expert'=8] {'expert'}, dimensions={1} | all-to-all | bytes 811008 | tf_op jit(solution)/shard_map/all_to_all | solution.py:41
  27.3 0.6 fusion.36
  27.9 0.1 squeeze.15
  28.1 0.1 squeeze.16
  28.2 0.8 pad_maximum_fusion.1
  29.0 0.0 all-gather.2.cloned.1.call-update
  29.0 0.0 reduce-scatter.4.cloned.1.call-start
  29.1 106.1 %all-gather.2.cloned.1.call-done = bf16[32,33,6144]{2,1,0:T(8,128)(2,1)} async-done(((bf16[1,33,6144]{2,1,0:T(8,128)(2,1)}), bf16[32,33,6144]{2,1,0:T(8,128)(2,1)}) %all-gather.2.cloned.1.call-update) | async-done | bytes 12976144 | tf_op jit(solution)/shard_map/all_gather | solution.py:44
  135.2 11.0 %fusion.35 = (bf16[32,33,3072]{2,1,0:T(8,128)(2,1)}, bf16[32,33,3072]{2,1,0:T(8,128)(2,1)}) fusion(bf16[32,33,6144]{2,1,0:T(8,128)(2,1)} %all-gather.2.cloned.1.call-done), kind=kLoop, calls=%fused_computation.64 | loop fusion | bytes 25952256 | tf_op jit(solution)/shard_map/slice | solution.py:49
  146.2 7.1 %reshape.64 = bf16[1056,3072]{1,0:T(8,128)(2,1)} reshape(bf16[32,33,3072]{2,1,0:T(8,128)(2,1)} %get-tuple-element.6) | data formatting | bytes 12976128 | tf_op jit(solution)/shard_map/reshape | solution.py:48
  153.3 5.3 %fusion.8 = f32[1056,256]{1,0:T(8,128)S(1)} fusion(bf16[1056,3072]{1,0:T(8,128)(2,1)} %reshape.64, bf16[1,3072,256]{2,1,0:T(8,128)(2,1)} %param.11), kind=kOutput, calls=%fused_computation.12 | convolution fusion | flops 1660944384 | bytes 9142272 | tf_op jit(solution)/shard_map/dot_general | solution.py:54
  158.6 0.3 copy-done.2
  158.8 2.9 multiply_convert_fusion.2
  161.8 1.9 convolution_convert_fusion
  163.6 4.3 %copy.49 = bf16[132,8,8,384]{3,2,1,0:T(8,128)(2,1)} copy(bf16[132,8,8,384]{3,1,2,0:T(8,128)(2,1)S(1)} %bitcast.65) | data formatting | bytes 12976128
  168.0 0.0 reduce-scatter.4.cloned.1.call-update
  168.0 7.1 %reshape.67 = bf16[1056,3072]{1,0:T(8,128)(2,1)} reshape(bf16[32,33,3072]{2,1,0:T(8,128)(2,1)} %get-tuple-element.5) | data formatting | bytes 12976128 | tf_op jit(solution)/shard_map/reshape | solution.py:49
  175.1 4.9 %fusion.3 = f32[1056,256]{1,0:T(8,128)S(1)} fusion(bf16[1056,3072]{1,0:T(8,128)(2,1)} %reshape.67, bf16[1,256,3072]{2,1,0:T(8,128)(2,1)S(1)} %copy-done), kind=kOutput, calls=%fused_computation.7 | convolution fusion | flops 1660944384 | bytes 9142272 | tf_op jit(solution)/shard_map/rd,fd->rf/dot_general | solution.py:60
  180.0 0.0 copy-start.4
  180.0 6.5 %fusion.1 = bf16[1,3072,256]{2,1,0:T(8,128)(2,1)} fusion(bf16[1056,3072]{1,0:T(8,128)(2,1)} %reshape.64, f32[1056,256]{1,0:T(8,128)S(1)} %fusion.3, f32[1056,256]{1,0:T(8,128)S(1)} %fusion.8), kind=kOutput, calls=%fused_computation.5 | convolution fusion | flops 1663352832 | bytes 10223616 | tf_op jit(solution)/shard_map/rd,rf->df/dot_general | solution.py:71
  186.6 3.6 %fusion = bf16[1,3072,256]{2,1,0:T(8,128)(2,1)} fusion(bf16[1056,3072]{1,0:T(8,128)(2,1)S(1)} %bitcast.68, f32[1056,256]{1,0:T(8,128)S(1)} %fusion.8, f32[1056,256]{1,0:T(8,128)S(1)} %fusion.3, f32[1056,256]{1,0:T(8,128)S(1)} %copy-done.4), kind=kOutput, calls=%fused_computation.4 | convolution fusion | flops 1664434176 | bytes 11304960 | tf_op jit(solution)/shard_map/rd,rf->df/dot_general | solution.py:68
  190.3 92.1 %reduce-scatter.4.cloned.1.call-done = bf16[1,8,33,384]{3,1,2,0:T(8,128)(2,1)} async-done(((bf16[32,8,33,384]{3,1,2,0:T(8,128)(2,1)}), bf16[1,8,33,384]{3,1,2,0:T(8,128)(2,1)}) %reduce-scatter.4.cloned.1.call-update) | async-done | bytes 202768
  282.3 1.6 copy.48
  284.0 4.7 %all-to-all-start.1 = ((bf16[1,8,33,384]{3,2,0,1:T(8,128)(2,1)}), bf16[1,8,33,384]{3,2,0,1:T(8,128)(2,1)S(1)}, u32[]{:S(2)}, u32[]{:S(2)}) async-start(bf16[1,8,33,384]{3,2,0,1:T(8,128)(2,1)} %copy.48), calls=%async_computation.1 | async-start | bytes 491520 | tf_op jit(solution)/shard_map/all_to_all | solution.py:77
  288.7 6.3 %fusion.2 = bf16[1,256,3072]{2,1,0:T(8,128)(2,1)} fusion(bf16[1056,256]{1,0:T(8,128)(2,1)S(1)} %get-tuple-element.13, bf16[1056,3072]{1,0:T(8,128)(2,1)} %reshape.67), kind=kOutput, calls=%fused_computation.6 | convolution fusion | flops 1661730816 | bytes 8601600 | tf_op jit(solution)/shard_map/rf,rd->fd/dot_general | solution.py:61
  295.0 0.1 reshape.66
  295.0 0.4 fusion.11
  295.4 0.4 fusion.10
  295.8 1.1 convolution_convert_fusion.6
  296.9 18.0 %psum.7 = f32[128,2]{0,1:T(2,128)} all-reduce(f32[128,2]{0,1:T(2,128)S(1)} %pad_maximum_fusion.2), channel_id=1, replica_groups=mesh['dpo'=16,'core'=2,'expert'=8] {'expert'}, use_global_device_ids=true, to_apply=%region_6.7 | all-reduce | flops 256 | bytes 2048 | tf_op jit(solution)/shard_map/psum | solution.py:88
  (20 shorter events, 0.1 us)
Async XLA Ops:
  7.2 154.6 %copy-start = (bf16[1,256,3072]{2,1,0:T(8,128)(2,1)S(1)}, bf16[1,256,3072]{2,1,0:T(8,128)(2,1)}, u32[]{:S(2)}) copy-start(bf16[1,256,3072]{2,1,0:T(8,128)(2,1)} %param.13) | copy-start | bytes 4718596
  7.2 128.0 %all-gather.2.cloned.1.call-start = ((), (), s32[]{:S(2)}) async-start(), calls=%async_computation.3 | async-start | bytes 16220160 | tf_op jit(solution)/shard_map/all_gather | solution.py:44
  29.0 253.3 %reduce-scatter.4.cloned.1.call-start = ((), (), s32[]{:S(2)}) async-start(), calls=%async_computation.4 | async-start | bytes 6690816
  153.3 5.3 %copy-start.1 = (bf16[1056,3072]{1,0:T(8,128)(2,1)S(1)}, bf16[1056,3072]{1,0:T(8,128)(2,1)}, u32[]{:S(2)}) copy-start(bf16[1056,3072]{1,0:T(8,128)(2,1)} %reshape.64) | copy-start | bytes 19464196
  153.3 5.6 %copy-start.2 = (bf16[1,3072,256]{2,1,0:T(8,128)(2,1)S(1)}, bf16[1,3072,256]{2,1,0:T(8,128)(2,1)}, u32[]{:S(2)}) copy-start(bf16[1,3072,256]{2,1,0:T(8,128)(2,1)} %param.12) | copy-start | bytes 4718596
  175.1 11.4 %slice-start = ((s8[6488064]{0:T(1024)(128)(4,1)}), s8[4194304]{0:T(1024)(128)(4,1)S(1)}, s32[]{:S(2)}) async-start(s8[6488064]{0:T(1024)(128)(4,1)} %bitcast.67), calls=%async_computation.5 | async-start | bytes 8388608
  180.0 6.6 %slice-start.1 = ((s8[6488064]{0:T(1024)(128)(4,1)}), s8[2293760]{0:T(1024)(128)(4,1)S(1)}, s32[]{:S(2)}) async-start(s8[6488064]{0:T(1024)(128)(4,1)} %bitcast.67), calls=%async_computation.6 | async-start | bytes 4587520
  180.0 6.6 %copy-start.4 = (f32[1056,256]{1,0:T(8,128)S(1)}, f32[1056,256]{1,0:T(8,128)}, u32[]{:S(2)}) copy-start(f32[1056,256]{1,0:T(8,128)} %get-tuple-element.14) | copy-start | bytes 3244036
  284.0 11.0 %all-to-all-start.1 = ((bf16[1,8,33,384]{3,2,0,1:T(8,128)(2,1)}), bf16[1,8,33,384]{3,2,0,1:T(8,128)(2,1)S(1)}, u32[]{:S(2)}, u32[]{:S(2)}) async-start(bf16[1,8,33,384]{3,2,0,1:T(8,128)(2,1)} %copy.48), calls=%async_computation.1 | async-start | bytes 491520 | tf_op jit(solution)/shard_map/all_to_all | solution.py:77
  288.7 6.3 %copy-start.3 = (bf16[128,384]{1,0:T(8,128)(2,1)S(1)}, bf16[128,384]{1,0:T(8,128)(2,1)}, u32[]{:S(2)}) copy-start(bf16[128,384]{1,0:T(8,128)(2,1)} %param.8) | copy-start | bytes 294916
Sparse Core Ops, SparseCore 0:
  29.2 105.9 all-gather.1
  168.1 114.1 reduce-scatter.3

commit v5 on v4

--- a/solution.py
+++ b/solution.py
@@ -45,8 +45,9 @@
     n_blk = blocks_all.shape[0]
     d_all = recv.shape[-1]
     n_rows = n_blk * capacity
-    gathered = blocks_all[:, :, :d_all].reshape(n_rows, d_all)
-    grads_in = blocks_all[:, :, d_all:].reshape(n_rows, d_all)
+    flat_all = blocks_all.reshape(n_rows, 2 * d_all)
+    gathered = flat_all[:, :d_all]
+    grads_in = flat_all[:, d_all:]
     gate_slab = w_gate[0]
     up_slab = w_up[0]
     down_slab = w_down[0]

time: 323 us -> 317 us (0.981)
  local copies, waits for them, and re-layouts: 35.4 us -> 23.8 us
  waiting for transfers between devices: 198 us -> 205 us
    slice x2 -> x1, local copies, waits for them, and re-layouts: 11.2 us -> 0.21 us  [the longest x1 11 us: local(): grads_in = blocks_all[:, :, d_all:].reshape(n_rows, d_all)]
    unnamed x3, waiting for transfers between devices: 92.1 us -> 98.7 us
    reshape x2 -> x1, local copies, waits for them, and re-layouts: 14.2 us -> 11.8 us  [local(): flat_all = blocks_all.reshape(n_rows, 2 * d_all)]
    unnamed x16 -> x24, local copies, waits for them, and re-layouts: 5.56 us -> 7.4 us
  transfers between devices with their start and end apart: 3 -> 3, of which waited for: 2 -> 2; matrix products, arithmetic and copies ran while one was open for 9% -> 7% of each run, Pallas kernels for 0% -> 0%
where the time goes in v5:
time: 317 us; the launch traced here: 316 us
  waiting for transfers between devices  205 us (65%)
  matrix products  34.5 us (11%)
  blocking collectives  31.2 us (10%)
  local copies, waits for them, and re-layouts  23.8 us (8%)
  between operations  14.3 us (5%)
  starting transfers between devices  4.98 us (2%)
    all_gather x1, waiting for transfers between devices, local(): blocks_all = lax.all_gather(both, DP, axis=0, tiled=True)  106 us
    unnamed x3, waiting for transfers between devices  98.7 us
    psum x1, blocking collectives, local(): d_route = lax.psum(partial_dots, 'expert')  18 us
    all_to_all x1, blocking collectives, local(): lax.all_to_all(sent, 'expert', split_axis=1, concat_axis=3, tiled=True)  13.2 us
    reshape x1, local copies, waits for them, and re-layouts, local(): flat_all = blocks_all.reshape(n_rows, 2 * d_all)  11.8 us
    unnamed x24, local copies, waits for them, and re-layouts  7.4 us
    dot_general x1, matrix products, local(): jnp.einsum('rd,rf->df', gathered, d_up_act, preferred_element_type=jnp.fl...  6.56 us
  transfers between devices with their start and end apart: 3, of which 2 were waited for; matrix products, arithmetic and copies ran while one was open for 7% of the time, Pallas kernels for 0%

profile of v5, /device:TPU:2, one launch (start us, length us, event | category | flops | bytes accessed | tf_op | source)
XLA Modules:
  0.0 315.9 jit_solution(15041428145175440626)
XLA Ops:
  7.2 0.0 copy-start
  7.2 0.0 all-gather.2.cloned.1.call-start
  7.2 0.9 copy.42
  8.1 0.1 eq.60
  8.3 0.1 eq.56
  8.4 0.8 slice_bitcast_fusion.2
  9.2 0.6 reduce-window.6
  9.7 0.2 slice_reduce_fusion
  10.0 0.1 fusion.53
  10.1 0.1 reshape.58
  10.2 0.1 copy.44
  10.3 0.7 multiply_add_fusion
  11.0 1.1 convolution_convert_fusion.2
  12.1 0.1 reshape.59
  12.2 1.3 convolution_convert_fusion.1
  13.5 0.1 reshape.60
  13.6 0.1 pad_maximum_fusion
  13.6 0.4 copy.45
  14.1 13.2 %all_to_all.24 = bf16[2,8,33,384]{3,0,2,1:T(2,128)(2,1)S(1)} all-to-all(bf16[2,8,33,384]{3,0,2,1:T(2,128)(2,1)S(1)} %copy.45), channel_id=1, replica_groups=mesh['dpo'=16,'core'=2,'expert'=8] {'expert'}, dimensions={1} | all-to-all | bytes 811008 | tf_op jit(solution)/shard_map/all_to_all | solution.py:41
  27.3 0.6 fusion.59
  27.9 0.1 squeeze.15
  28.1 0.1 squeeze.16
  28.2 0.8 pad_maximum_fusion.1
  29.0 0.0 all-gather.2.cloned.1.call-update
  29.0 0.0 copy-start.2
  29.0 0.0 reduce-scatter.4.cloned.1.call-start
  29.1 106.1 %all-gather.2.cloned.1.call-done = bf16[32,33,6144]{2,1,0:T(8,128)(2,1)} async-done(((bf16[1,33,6144]{2,1,0:T(8,128)(2,1)}), bf16[32,33,6144]{2,1,0:T(8,128)(2,1)}) %all-gather.2.cloned.1.call-update) | async-done | bytes 12976144 | tf_op jit(solution)/shard_map/all_gather | solution.py:44
  135.2 11.8 %reshape.61 = bf16[1056,6144]{1,0:T(8,128)(2,1)} reshape(bf16[32,33,6144]{2,1,0:T(8,128)(2,1)} %all-gather.2.cloned.1.call-done) | data formatting | bytes 25952256 | tf_op jit(solution)/shard_map/reshape | solution.py:48
  147.0 4.8 %fusion.10 = f32[1056,256]{1,0:T(8,128)S(1)} fusion(bf16[1056,6144]{1,0:T(8,128)(2,1)} %reshape.61, bf16[1,3072,256]{2,1,0:T(8,128)(2,1)S(1)} %copy-done.2), kind=kOutput, calls=%fused_computation.11 | convolution fusion | flops 1660944384 | bytes 9142272 | tf_op jit(solution)/shard_map/dot_general | solution.py:55
  151.9 1.7 copy-done.1
  153.6 0.4 copy-done.3
  154.0 1.9 multiply_convert_fusion.2
  155.9 1.9 convolution_convert_fusion
  157.8 4.4 %copy.49 = bf16[132,8,8,384]{3,2,1,0:T(8,128)(2,1)} copy(bf16[132,8,8,384]{3,1,2,0:T(8,128)(2,1)S(1)} %bitcast.59) | data formatting | bytes 12976128
  162.1 0.0 reduce-scatter.4.cloned.1.call-update
  162.1 0.0 copy-start.6
  162.2 4.9 %fusion.2 = f32[1056,256]{1,0:T(8,128)S(1)} fusion(bf16[1056,6144]{1,0:T(8,128)(2,1)} %reshape.61, bf16[1,256,3072]{2,1,0:T(8,128)(2,1)S(1)} %copy-done), kind=kOutput, calls=%fused_computation.3 | convolution fusion | flops 1660944384 | bytes 9142272 | tf_op jit(solution)/shard_map/rd,fd->rf/dot_general | solution.py:61
  167.1 6.6 %fusion.24 = bf16[1,3072,256]{2,1,0:T(8,128)(2,1)} fusion(bf16[1056,6144]{1,0:T(8,128)(2,1)} %reshape.61, f32[1056,256]{1,0:T(8,128)S(1)} %fusion.2, f32[1056,256]{1,0:T(8,128)S(1)} %copy-done.6), kind=kOutput, calls=%fused_computation.17 | convolution fusion | flops 1663352832 | bytes 10223616 | tf_op jit(solution)/shard_map/rd,rf->df/dot_general | solution.py:72
  173.7 4.0 %fusion.27 = bf16[1,3072,256]{2,1,0:T(8,128)(2,1)} fusion(bf16[1056,6144]{1,0:T(8,128)(2,1)S(1)} %bitcast.62, f32[1056,256]{1,0:T(8,128)S(1)} %copy-done.6, f32[1056,256]{1,0:T(8,128)S(1)} %fusion.2, f32[1056,256]{1,0:T(8,128)S(1)} %get-tuple-element.12), kind=kOutput, calls=%fused_computation.18 | convolution fusion | flops 1664434176 | bytes 11304960 | tf_op jit(solution)/shard_map/rd,rf->df/dot_general | solution.py:69
  177.7 98.6 %reduce-scatter.4.cloned.1.call-done = bf16[1,8,33,384]{3,1,2,0:T(8,128)(2,1)} async-done(((bf16[32,8,33,384]{3,1,2,0:T(8,128)(2,1)}), bf16[1,8,33,384]{3,1,2,0:T(8,128)(2,1)}) %reduce-scatter.4.cloned.1.call-update) | async-done | bytes 202768
  276.3 1.6 copy.48
  278.0 4.9 %all-to-all-start.1 = ((bf16[1,8,33,384]{3,2,0,1:T(8,128)(2,1)}), bf16[1,8,33,384]{3,2,0,1:T(8,128)(2,1)S(1)}, u32[]{:S(2)}, u32[]{:S(2)}) async-start(bf16[1,8,33,384]{3,2,0,1:T(8,128)(2,1)} %copy.48), calls=%async_computation.1 | async-start | bytes 491520 | tf_op jit(solution)/shard_map/all_to_all | solution.py:78
  282.9 6.3 %fusion.21 = bf16[1,256,3072]{2,1,0:T(8,128)(2,1)} fusion(bf16[1056,256]{1,0:T(8,128)(2,1)S(1)} %get-tuple-element.11, bf16[1056,6144]{1,0:T(8,128)(2,1)} %reshape.61), kind=kOutput, calls=%fused_computation.16 | convolution fusion | flops 1661730816 | bytes 8601600 | tf_op jit(solution)/shard_map/rf,rd->fd/dot_general | solution.py:62
  289.1 0.1 reshape.63
  289.2 0.4 fusion.35
  289.6 0.4 fusion.34
  290.0 1.1 convolution_convert_fusion.3
  291.1 18.0 %psum.7 = f32[128,2]{0,1:T(2,128)} all-reduce(f32[128,2]{0,1:T(2,128)S(1)} %pad_maximum_fusion.2), channel_id=1, replica_groups=mesh['dpo'=16,'core'=2,'expert'=8] {'expert'}, use_global_device_ids=true, to_apply=%region_6.7 | all-reduce | flops 256 | bytes 2048 | tf_op jit(solution)/shard_map/psum | solution.py:89
  (26 shorter events, 0.2 us)
Async XLA Ops:
  7.2 148.7 %copy-start = (bf16[1,256,3072]{2,1,0:T(8,128)(2,1)S(1)}, bf16[1,256,3072]{2,1,0:T(8,128)(2,1)}, u32[]{:S(2)}) copy-start(bf16[1,256,3072]{2,1,0:T(8,128)(2,1)} %param.13) | copy-start | bytes 4718596
  7.2 128.0 %all-gather.2.cloned.1.call-start = ((), (), s32[]{:S(2)}) async-start(), calls=%async_computation.3 | async-start | bytes 16220160 | tf_op jit(solution)/shard_map/all_gather | solution.py:44
  29.0 118.0 %copy-start.2 = (bf16[1,3072,256]{2,1,0:T(8,128)(2,1)S(1)}, bf16[1,3072,256]{2,1,0:T(8,128)(2,1)}, u32[]{:S(2)}) copy-start(bf16[1,3072,256]{2,1,0:T(8,128)(2,1)} %param.11) | copy-start | bytes 4718596
  29.0 247.3 %reduce-scatter.4.cloned.1.call-start = ((), (), s32[]{:S(2)}) async-start(), calls=%async_computation.4 | async-start | bytes 6690816
  147.0 6.5 %copy-start.1 = (bf16[1056,6144]{1,0:T(8,128)(2,1)S(1)}, bf16[1056,6144]{1,0:T(8,128)(2,1)}, u32[]{:S(2)}) copy-start(bf16[1056,6144]{1,0:T(8,128)(2,1)} %reshape.61) | copy-start | bytes 38928388
  147.0 7.0 %copy-start.3 = (bf16[1,3072,256]{2,1,0:T(8,128)(2,1)S(1)}, bf16[1,3072,256]{2,1,0:T(8,128)(2,1)}, u32[]{:S(2)}) copy-start(bf16[1,3072,256]{2,1,0:T(8,128)(2,1)} %param.12) | copy-start | bytes 4718596
  154.0 1.9 copy-start.5
  162.1 4.9 %copy-start.6 = (f32[1056,256]{1,0:T(8,128)S(1)}, f32[1056,256]{1,0:T(8,128)}, u32[]{:S(2)}) copy-start(f32[1056,256]{1,0:T(8,128)} %copy-done.5) | copy-start | bytes 3244036
  162.1 11.5 %slice-start = ((s8[12976128]{0:T(1024)(128)(4,1)}), s8[4194304]{0:T(1024)(128)(4,1)S(1)}, s32[]{:S(2)}) async-start(s8[12976128]{0:T(1024)(128)(4,1)} %bitcast.61), calls=%async_computation.5 | async-start | bytes 8388608
  162.2 11.5 %slice-start.1 = ((s8[12976128]{0:T(1024)(128)(4,1)}), s8[4194304]{0:T(1024)(128)(4,1)S(1)}, s32[]{:S(2)}) async-start(s8[12976128]{0:T(1024)(128)(4,1)} %bitcast.61), calls=%async_computation.6 | async-start | bytes 8388608
  167.1 6.6 %slice-start.2 = ((s8[12976128]{0:T(1024)(128)(4,1)}), s8[4194304]{0:T(1024)(128)(4,1)S(1)}, s32[]{:S(2)}) async-start(s8[12976128]{0:T(1024)(128)(4,1)} %bitcast.61), calls=%async_computation.7 | async-start | bytes 8388608
  167.1 6.6 %slice-start.3 = ((s8[12976128]{0:T(1024)(128)(4,1)}), s8[393216]{0:T(1024)(128)(4,1)S(1)}, s32[]{:S(2)}) async-start(s8[12976128]{0:T(1024)(128)(4,1)} %bitcast.61), calls=%async_computation.8 | async-start | bytes 786432
  278.0 11.2 %all-to-all-start.1 = ((bf16[1,8,33,384]{3,2,0,1:T(8,128)(2,1)}), bf16[1,8,33,384]{3,2,0,1:T(8,128)(2,1)S(1)}, u32[]{:S(2)}, u32[]{:S(2)}) async-start(bf16[1,8,33,384]{3,2,0,1:T(8,128)(2,1)} %copy.48), calls=%async_computation.1 | async-start | bytes 491520 | tf_op jit(solution)/shard_map/all_to_all | solution.py:78
  282.9 6.3 %copy-start.4 = (bf16[128,384]{1,0:T(8,128)(2,1)S(1)}, bf16[128,384]{1,0:T(8,128)(2,1)}, u32[]{:S(2)}) copy-start(bf16[128,384]{1,0:T(8,128)(2,1)} %param.8) | copy-start | bytes 294916
Sparse Core Ops, SparseCore 0:
  29.1 105.9 all-gather.1
  162.3 114.0 reduce-scatter.3

commit v6 on v5

--- a/solution.py
+++ b/solution.py
@@ -37,7 +37,9 @@
     sent_tokens = sent_tokens.astype(jnp.bfloat16).reshape(1, experts, capacity, feat)
     sent_grads = jnp.dot(weighted, out_grad.astype(jnp.float32), precision=highest)
     sent_grads = sent_grads.astype(jnp.bfloat16).reshape(1, experts, capacity, feat)
-    sent = jnp.concatenate([sent_tokens, sent_grads], axis=0)
+    sent_raw = jnp.dot(dispatch.astype(jnp.bfloat16), out_grad, preferred_element_type=jnp.float32)
+    sent_raw = sent_raw.astype(jnp.bfloat16).reshape(1, experts, capacity, feat)
+    sent = jnp.concatenate([sent_tokens, sent_grads, sent_raw], axis=0)
     recv = lax.all_to_all(sent, "expert", split_axis=1, concat_axis=3, tiled=True)
 
     both = jnp.concatenate([recv[0], recv[1]], axis=-1)
@@ -75,18 +77,24 @@
 
     blocks = partial_out.reshape(n_blk, capacity, experts, d_all // experts).transpose(0, 2, 1, 3)
     summed_out = lax.psum_scatter(blocks, DP, scatter_dimension=0, tiled=True)
-    returned_out = lax.all_to_all(summed_out, "expert", split_axis=1, concat_axis=0, tiled=True)
+    raw_rows = recv[2, 0].reshape(capacity, experts, d_all // experts).astype(jnp.float32)
+    dots = jnp.einsum("cfj,fcj->c", raw_rows, summed_out[0].astype(jnp.float32), precision=highest)
+    hi = lax.reduce_precision(dots, exponent_bits=8, mantissa_bits=7)
+    rest = dots - hi
+    mid = lax.reduce_precision(rest, exponent_bits=8, mantissa_bits=7)
+    lo = rest - mid
+    pieces = jnp.stack([hi, mid, lo], axis=1).astype(jnp.bfloat16)
+    lanes = jnp.pad(pieces, ((0, 0), (0, 128 - pieces.shape[1])))
+    lanes = jnp.broadcast_to(lanes[None, None], (1, experts) + lanes.shape)
+    payload = jnp.concatenate([summed_out, lanes], axis=-1)
+    returned = lax.all_to_all(payload, "expert", split_axis=1, concat_axis=0, tiled=True)
+    returned_out = returned[..., : d_all // experts]
+    got = returned[..., d_all // experts : d_all // experts + 3].astype(jnp.float32)
+    dots_all = ((got[..., 0] + got[..., 1]) + got[..., 2]).reshape(-1)
     flat_out = returned_out.reshape(experts * capacity, -1).astype(jnp.float32)
     combined = jnp.dot(weighted.T, flat_out, precision=highest).astype(jnp.bfloat16)
-    grads32 = out_grad.astype(jnp.float32)
-    partial_dots = jnp.stack(
-        [
-            jnp.sum(grads32 * jnp.dot(picks[which].T, flat_out, precision=highest), axis=1)
-            for which in range(top_count)
-        ],
-        axis=1,
-    )
-    d_route = lax.psum(partial_dots, "expert")
+    target = expert_ids * capacity + slot_table(expert_ids, experts)
+    d_route = dots_all[target]
     return (combined, d_gate[None], d_up[None], d_down[None], d_route)
 
 

time: 317 us -> 307 us (0.968)
  blocking collectives: 31.2 us -> 16.7 us
    psum x1 -> x0, blocking collectives: 18 us -> none  [local(): d_route = lax.psum(partial_dots, 'expert')]
    all_to_all x1, blocking collectives: 13.2 us -> 16.7 us  [local(): lax.all_to_all(sent, 'expert', split_axis=1, concat_axis=3, tiled=True)]
    unnamed x24 -> x26, local copies, waits for them, and re-layouts: 7.4 us -> 8.19 us
where the time goes in v6:
time: 307 us; the launch traced here: 306 us
  waiting for transfers between devices  205 us (67%)
  matrix products  35.2 us (11%)
  local copies, waits for them, and re-layouts  25.4 us (8%)
  blocking collectives  16.7 us (5%)
  between operations  14.4 us (5%)
  other arithmetic  4.92 us (2%)
  starting transfers between devices  4.86 us (2%)
    all_gather x1, waiting for transfers between devices, local(): blocks_all = lax.all_gather(both, DP, axis=0, tiled=True)  106 us
    unnamed x3, waiting for transfers between devices  98.7 us
    all_to_all x1, blocking collectives, local(): lax.all_to_all(sent, 'expert', split_axis=1, concat_axis=3, tiled=True)  16.7 us
    reshape x1, local copies, waits for them, and re-layouts, local(): flat_all = blocks_all.reshape(n_rows, 2 * d_all)  11.8 us
    unnamed x26, local copies, waits for them, and re-layouts  8.19 us
    dot_general x1, matrix products, local(): jnp.einsum('rd,rf->df', gathered, d_up_act, preferred_element_type=jnp.fl...  6.51 us
    dot_general x1, matrix products, local(): jnp.einsum('rf,rd->fd', hidden, grads_in, preferred_element_type=jnp.floa...  6.28 us
  transfers between devices with their start and end apart: 3, of which 2 were waited for; matrix products, arithmetic and copies ran while one was open for 7% of the time, Pallas kernels for 0%

profile of v6, /device:TPU:2, one launch (start us, length us, event | category | flops | bytes accessed | tf_op | source)
XLA Modules:
  0.0 306.3 jit_solution(1663517891706048601)
XLA Ops:
  7.2 0.9 copy.51
  8.1 0.1 eq.67
  8.3 0.1 eq.63
  8.4 0.6 reduce-window.6
  9.0 0.2 slice_reduce_fusion
  9.3 0.1 fusion.53
  9.4 0.1 reshape.80
  9.6 0.7 compare_select_fusion
  10.3 1.1 convolution_convert_fusion.1
  11.4 0.1 reshape.83
  11.5 0.8 slice_bitcast_fusion.3
  12.2 1.3 convolution_convert_fusion.2
  13.5 0.1 reshape.82
  13.6 0.2 convolution_convert_fusion.3
  13.8 0.1 reshape.81
  13.9 0.1 pad_maximum_fusion
  14.1 16.7 %all_to_all.27 = bf16[3,8,33,384]{3,2,0,1:T(8,128)(2,1)S(1)} all-to-all(bf16[3,8,33,384]{3,2,0,1:T(8,128)(2,1)S(1)} %copy.54), channel_id=1, replica_groups=mesh['dpo'=16,'core'=2,'expert'=8] {'expert'}, dimensions={1} | all-to-all | bytes 1216512 | tf_op jit(solution)/shard_map/all_to_all | solution.py:43
  30.8 0.1 fusion.63
  30.9 0.1 squeeze.22
  31.1 0.1 squeeze.21
  31.2 0.8 pad_maximum_fusion.1
  32.1 106.2 %all-gather.2.cloned.1.call-done = bf16[32,33,6144]{2,1,0:T(8,128)(2,1)} async-done(((bf16[1,33,6144]{2,1,0:T(8,128)(2,1)}), bf16[32,33,6144]{2,1,0:T(8,128)(2,1)}) %all-gather.2.cloned.1.call-update) | async-done | bytes 12976144 | tf_op jit(solution)/shard_map/all_gather | solution.py:46
  138.3 11.8 %reshape.84 = bf16[1056,6144]{1,0:T(8,128)(2,1)} reshape(bf16[32,33,6144]{2,1,0:T(8,128)(2,1)} %all-gather.2.cloned.1.call-done) | data formatting | bytes 25952256 | tf_op jit(solution)/shard_map/reshape | solution.py:50
  150.1 5.3 %fusion.10 = f32[1056,256]{1,0:T(8,128)S(1)} fusion(bf16[1056,6144]{1,0:T(8,128)(2,1)} %reshape.84, bf16[1,3072,256]{2,1,0:T(8,128)(2,1)} %param.11), kind=kOutput, calls=%fused_computation.12 | convolution fusion | flops 1660944384 | bytes 9142272 | tf_op jit(solution)/shard_map/dot_general | solution.py:57
  155.4 1.7 copy-done.1
  157.1 0.4 copy-done.3
  157.5 2.9 multiply_convert_fusion.2
  160.4 1.9 convolution_convert_fusion
  162.3 4.4 %copy.67 = bf16[132,8,8,384]{3,2,1,0:T(8,128)(2,1)} copy(bf16[132,8,8,384]{3,1,2,0:T(8,128)(2,1)S(1)} %bitcast.71) | data formatting | bytes 12976128
  166.7 0.1 copy.59
  166.8 0.1 reshape.89
  167.0 4.9 %fusion.2 = f32[1056,256]{1,0:T(8,128)S(1)} fusion(bf16[1056,6144]{1,0:T(8,128)(2,1)} %reshape.84, bf16[1,256,3072]{2,1,0:T(8,128)(2,1)S(1)} %copy-done), kind=kOutput, calls=%fused_computation.4 | convolution fusion | flops 1660944384 | bytes 9142272 | tf_op jit(solution)/shard_map/rd,fd->rf/dot_general | solution.py:63
  171.9 6.5 %fusion.24 = bf16[1,3072,256]{2,1,0:T(8,128)(2,1)} fusion(bf16[1056,6144]{1,0:T(8,128)(2,1)} %reshape.84, f32[1056,256]{1,0:T(8,128)S(1)} %fusion.2, f32[1056,256]{1,0:T(8,128)S(1)} %copy-done.5), kind=kOutput, calls=%fused_computation.18 | convolution fusion | flops 1663352832 | bytes 10223616 | tf_op jit(solution)/shard_map/rd,rf->df/dot_general | solution.py:74
  178.5 3.8 %fusion.27 = bf16[1,3072,256]{2,1,0:T(8,128)(2,1)} fusion(bf16[1056,6144]{1,0:T(8,128)(2,1)S(1)} %bitcast.74, f32[1056,256]{1,0:T(8,128)S(1)} %copy-done.5, f32[1056,256]{1,0:T(8,128)S(1)} %fusion.2, f32[1056,256]{1,0:T(8,128)S(1)} %copy-done.6), kind=kOutput, calls=%fused_computation.19 | convolution fusion | flops 1664434176 | bytes 11304960 | tf_op jit(solution)/shard_map/rd,rf->df/dot_general | solution.py:71
  182.3 98.7 %reduce-scatter.4.cloned.1.call-done = bf16[1,8,33,384]{3,1,2,0:T(8,128)(2,1)} async-done(((bf16[32,8,33,384]{3,1,2,0:T(8,128)(2,1)}), bf16[1,8,33,384]{3,1,2,0:T(8,128)(2,1)}) %reduce-scatter.4.cloned.1.call-update) | async-done | bytes 202768
  281.0 1.3 multiply_reduce_fusion
  282.3 0.1 copy.66
  282.4 1.0 pad_maximum_fusion.2
  283.4 0.8 copy.58
  284.2 4.8 %all-to-all-start.1 = ((bf16[1,8,33,512]{3,2,0,1:T(8,128)(2,1)}), bf16[1,8,33,512]{3,2,0,1:T(8,128)(2,1)S(1)}, u32[]{:S(2)}, u32[]{:S(2)}) async-start(bf16[1,8,33,512]{3,2,0,1:T(8,128)(2,1)} %copy.58), calls=%async_computation.1 | async-start | bytes 655360 | tf_op jit(solution)/shard_map/all_to_all | solution.py:90
  289.0 6.3 %fusion.21 = bf16[1,256,3072]{2,1,0:T(8,128)(2,1)} fusion(bf16[1056,256]{1,0:T(8,128)(2,1)S(1)} %get-tuple-element.42, bf16[1056,6144]{1,0:T(8,128)(2,1)} %reshape.84), kind=kOutput, calls=%fused_computation.17 | convolution fusion | flops 1661730816 | bytes 8601600 | tf_op jit(solution)/shard_map/rf,rd->fd/dot_general | solution.py:64
  295.3 0.1 reshape.86
  295.4 1.1 convolution_convert_fusion.4
  296.5 0.2 fusion.37
  296.7 0.1 add.49
  296.8 2.0 gather_fusion
  298.7 0.1 reshape.88
  298.9 0.6 copy.60
  (41 shorter events, 0.5 us)
Async XLA Ops:
  7.2 153.3 %copy-start = (bf16[1,256,3072]{2,1,0:T(8,128)(2,1)S(1)}, bf16[1,256,3072]{2,1,0:T(8,128)(2,1)}, u32[]{:S(2)}) copy-start(bf16[1,256,3072]{2,1,0:T(8,128)(2,1)} %param.13) | copy-start | bytes 4718596
  7.2 6.4 %copy-start.2 = (bf16[128,384]{1,0:T(8,128)(2,1)S(1)}, bf16[128,384]{1,0:T(8,128)(2,1)}, u32[]{:S(2)}) copy-start(bf16[128,384]{1,0:T(8,128)(2,1)} %param.7) | copy-start | bytes 294916
  7.2 131.1 %all-gather.2.cloned.1.call-start = ((), (), s32[]{:S(2)}) async-start(), calls=%async_computation.3 | async-start | bytes 16220160 | tf_op jit(solution)/shard_map/all_gather | solution.py:46
  32.0 248.9 %reduce-scatter.4.cloned.1.call-start = ((), (), s32[]{:S(2)}) async-start(), calls=%async_computation.4 | async-start | bytes 6690816
  150.1 7.0 %copy-start.1 = (bf16[1056,6144]{1,0:T(8,128)(2,1)S(1)}, bf16[1056,6144]{1,0:T(8,128)(2,1)}, u32[]{:S(2)}) copy-start(bf16[1056,6144]{1,0:T(8,128)(2,1)} %reshape.84) | copy-start | bytes 38928388
  150.1 7.4 %copy-start.3 = (bf16[1,3072,256]{2,1,0:T(8,128)(2,1)S(1)}, bf16[1,3072,256]{2,1,0:T(8,128)(2,1)}, u32[]{:S(2)}) copy-start(bf16[1,3072,256]{2,1,0:T(8,128)(2,1)} %param.12) | copy-start | bytes 4718596
  157.5 2.9 copy-start.4
  167.0 4.9 %copy-start.5 = (f32[1056,256]{1,0:T(8,128)S(1)}, f32[1056,256]{1,0:T(8,128)}, u32[]{:S(2)}) copy-start(f32[1056,256]{1,0:T(8,128)} %copy-done.4) | copy-start | bytes 3244036
  167.0 11.5 %slice-start = ((s8[12976128]{0:T(1024)(128)(4,1)}), s8[4194304]{0:T(1024)(128)(4,1)S(1)}, s32[]{:S(2)}) async-start(s8[12976128]{0:T(1024)(128)(4,1)} %bitcast.73), calls=%async_computation.5 | async-start | bytes 8388608
  167.0 11.5 %slice-start.1 = ((s8[12976128]{0:T(1024)(128)(4,1)}), s8[4194304]{0:T(1024)(128)(4,1)S(1)}, s32[]{:S(2)}) async-start(s8[12976128]{0:T(1024)(128)(4,1)} %bitcast.73), calls=%async_computation.6 | async-start | bytes 8388608
  171.9 6.6 %slice-start.2 = ((s8[12976128]{0:T(1024)(128)(4,1)}), s8[4194304]{0:T(1024)(128)(4,1)S(1)}, s32[]{:S(2)}) async-start(s8[12976128]{0:T(1024)(128)(4,1)} %bitcast.73), calls=%async_computation.7 | async-start | bytes 8388608
  171.9 6.6 %slice-start.3 = ((s8[12976128]{0:T(1024)(128)(4,1)}), s8[393216]{0:T(1024)(128)(4,1)S(1)}, s32[]{:S(2)}) async-start(s8[12976128]{0:T(1024)(128)(4,1)} %bitcast.73), calls=%async_computation.8 | async-start | bytes 786432
  171.9 6.5 %copy-start.6 = (f32[1056,256]{1,0:T(8,128)S(1)}, f32[1056,256]{1,0:T(8,128)}, u32[]{:S(2)}) copy-start(f32[1056,256]{1,0:T(8,128)} %get-tuple-element.43) | copy-start | bytes 3244036
  284.2 11.1 %all-to-all-start.1 = ((bf16[1,8,33,512]{3,2,0,1:T(8,128)(2,1)}), bf16[1,8,33,512]{3,2,0,1:T(8,128)(2,1)S(1)}, u32[]{:S(2)}, u32[]{:S(2)}) async-start(bf16[1,8,33,512]{3,2,0,1:T(8,128)(2,1)} %copy.58), calls=%async_computation.1 | async-start | bytes 655360 | tf_op jit(solution)/shard_map/all_to_all | solution.py:90
Sparse Core Ops, SparseCore 0:
  32.2 106.0 all-gather.1
  166.8 114.1 reduce-scatter.3

commit v7 on v6

--- a/solution.py
+++ b/solution.py
@@ -76,7 +76,11 @@
     )
 
     blocks = partial_out.reshape(n_blk, capacity, experts, d_all // experts).transpose(0, 2, 1, 3)
-    summed_out = lax.psum_scatter(blocks, DP, scatter_dimension=0, tiled=True)
+    dj = d_all // experts
+    blocks = blocks.reshape(n_blk // n_core, n_core, experts, capacity, dj).transpose(1, 0, 2, 3, 4)
+    blocks = blocks.reshape(n_blk, experts, capacity, dj)
+    on_chip = lax.psum_scatter(blocks, "core", scatter_dimension=0, tiled=True)
+    summed_out = lax.psum_scatter(on_chip, "dpo", scatter_dimension=0, tiled=True)
     raw_rows = recv[2, 0].reshape(capacity, experts, d_all // experts).astype(jnp.float32)
     dots = jnp.einsum("cfj,fcj->c", raw_rows, summed_out[0].astype(jnp.float32), precision=highest)
     hi = lax.reduce_precision(dots, exponent_bits=8, mantissa_bits=7)

time: 307 us -> 320 us (1.042)
  waiting for transfers between devices: 205 us -> 218 us
    reduce_scatter x0 -> x1, waiting for transfers between devices: none -> 27.7 us  [local(): on_chip = lax.psum_scatter(blocks, 'core', scatter_dimension=0, tiled=True)]
    unnamed x3 -> x4, waiting for transfers between devices: 98.7 us -> 84 us
    transpose x0 -> x1, local copies, waits for them, and re-layouts: none -> 3.38 us  [local(): blocks.reshape(n_blk // n_core, n_core, experts, capacity, dj)]
    unnamed x26 -> x28, local copies, waits for them, and re-layouts: 8.19 us -> 5.45 us
  transfers between devices with their start and end apart: 3 -> 4, of which waited for: 2 -> 3; matrix products, arithmetic and copies ran while one was open for 7% -> 7% of each run, Pallas kernels for 0% -> 0%
where the time goes in v7:
time: 320 us
  waiting for transfers between devices  218 us (68%)
  matrix products  34.9 us (11%)
  local copies, waits for them, and re-layouts  26 us (8%)
  blocking collectives  16.7 us (5%)
  between operations  14.1 us (4%)
  starting transfers between devices  5.11 us (2%)
  other arithmetic  4.92 us (2%)
    all_gather x1, waiting for transfers between devices, local(): blocks_all = lax.all_gather(both, DP, axis=0, tiled=True)  106 us
    unnamed x4, waiting for transfers between devices  84 us
    reduce_scatter x1, waiting for transfers between devices, local(): on_chip = lax.psum_scatter(blocks, 'core', scatter_dimension=0, tiled=True)  27.7 us
    all_to_all x1, blocking collectives, local(): lax.all_to_all(sent, 'expert', split_axis=1, concat_axis=3, tiled=True)  16.7 us
    reshape x1, local copies, waits for them, and re-layouts, local(): flat_all = blocks_all.reshape(n_rows, 2 * d_all)  11.8 us
    dot_general x1, matrix products, local(): jnp.einsum('rd,rf->df', gathered, d_up_act, preferred_element_type=jnp.fl...  6.51 us
  transfers between devices with their start and end apart: 4, of which 3 were waited for; matrix products, arithmetic and copies ran while one was open for 7% of the time, Pallas kernels for 0%

profile of v7, /device:TPU:2, one launch (start us, length us, event | category | flops | bytes accessed | tf_op | source)
XLA Modules:
  0.0 319.7 jit_solution(13610513194046409011)
XLA Ops:
  7.2 0.9 copy.45
  8.1 0.1 eq.67
  8.3 0.1 eq.63
  8.4 0.6 reduce-window.6
  9.0 0.2 slice_reduce_fusion
  9.3 0.1 fusion.53
  9.4 0.1 reshape.86
  9.6 0.7 compare_select_fusion
  10.3 1.1 convolution_convert_fusion.1
  11.4 0.1 reshape.89
  11.5 0.8 slice_bitcast_fusion.3
  12.2 1.3 convolution_convert_fusion.2
  13.5 0.1 reshape.88
  13.6 0.2 convolution_convert_fusion.3
  13.9 0.1 pad_maximum_fusion
  14.1 16.7 %all_to_all.27 = bf16[3,8,33,384]{3,2,0,1:T(8,128)(2,1)S(1)} all-to-all(bf16[3,8,33,384]{3,2,0,1:T(8,128)(2,1)S(1)} %copy.48), channel_id=1, replica_groups=mesh['dpo'=16,'core'=2,'expert'=8] {'expert'}, dimensions={1} | all-to-all | bytes 1216512 | tf_op jit(solution)/shard_map/all_to_all | solution.py:43
  30.9 0.1 squeeze.22
  31.1 0.1 squeeze.21
  31.2 0.8 pad_maximum_fusion.1
  32.1 106.2 %all-gather.2.cloned.1.call-done = bf16[32,33,6144]{2,1,0:T(8,128)(2,1)} async-done(((bf16[1,33,6144]{2,1,0:T(8,128)(2,1)}), bf16[32,33,6144]{2,1,0:T(8,128)(2,1)}) %all-gather.2.cloned.1.call-update) | async-done | bytes 12976144 | tf_op jit(solution)/shard_map/all_gather | solution.py:46
  138.3 11.8 %reshape.90 = bf16[1056,6144]{1,0:T(8,128)(2,1)} reshape(bf16[32,33,6144]{2,1,0:T(8,128)(2,1)} %all-gather.2.cloned.1.call-done) | data formatting | bytes 25952256 | tf_op jit(solution)/shard_map/reshape | solution.py:50
  150.1 5.3 %fusion.10 = f32[1056,256]{1,0:T(8,128)S(1)} fusion(bf16[1056,6144]{1,0:T(8,128)(2,1)} %reshape.90, bf16[1,3072,256]{2,1,0:T(8,128)(2,1)} %param.11), kind=kOutput, calls=%fused_computation.12 | convolution fusion | flops 1660944384 | bytes 9142272 | tf_op jit(solution)/shard_map/dot_general | solution.py:57
  155.4 1.7 copy-done.2
  157.1 0.4 copy-done.4
  157.5 2.9 multiply_convert_fusion.2
  160.4 1.9 convolution_convert_fusion
  162.3 1.6 copy.62
  163.9 3.4 %copy.51 = bf16[2,16,8,33,384]{4,2,3,1,0:T(8,128)(2,1)} copy(bf16[2,16,8,33,384]{4,2,3,0,1:T(8,128)(2,1)S(1)} %bitcast.78) | data formatting | bytes 12976128 | tf_op jit(solution)/shard_map/transpose | solution.py:80
  167.3 0.2 reduce-scatter.7.cloned.1.call-start
  167.6 27.7 %reduce-scatter.5.cloned.1.call-done = bf16[16,8,33,384]{3,1,2,0:T(8,128)(2,1)} async-done(((bf16[32,8,33,384]{3,1,2,0:T(8,128)(2,1)}), bf16[16,8,33,384]{3,1,2,0:T(8,128)(2,1)}) %reduce-scatter.5.cloned.1.call-update) | async-done | bytes 3244048 | tf_op jit(solution)/shard_map/reduce_scatter | solution.py:82
  195.3 0.1 copy.54
  195.4 0.1 reshape.97
  195.6 4.9 %fusion.2 = f32[1056,256]{1,0:T(8,128)S(1)} fusion(bf16[1056,6144]{1,0:T(8,128)(2,1)} %reshape.90, bf16[1,256,3072]{2,1,0:T(8,128)(2,1)S(1)} %copy-done), kind=kOutput, calls=%fused_computation.4 | convolution fusion | flops 1660944384 | bytes 9142272 | tf_op jit(solution)/shard_map/rd,fd->rf/dot_general | solution.py:63
  200.5 6.5 %fusion.24 = bf16[1,3072,256]{2,1,0:T(8,128)(2,1)} fusion(bf16[1056,6144]{1,0:T(8,128)(2,1)} %reshape.90, f32[1056,256]{1,0:T(8,128)S(1)} %fusion.2, f32[1056,256]{1,0:T(8,128)S(1)} %copy-done.6), kind=kOutput, calls=%fused_computation.18 | convolution fusion | flops 1663352832 | bytes 10223616 | tf_op jit(solution)/shard_map/rd,rf->df/dot_general | solution.py:74
  207.1 3.6 %fusion.27 = bf16[1,3072,256]{2,1,0:T(8,128)(2,1)} fusion(bf16[1056,6144]{1,0:T(8,128)(2,1)S(1)} %bitcast.80, f32[1056,256]{1,0:T(8,128)S(1)} %copy-done.6, f32[1056,256]{1,0:T(8,128)S(1)} %fusion.2, f32[1056,256]{1,0:T(8,128)S(1)} %copy-done.7), kind=kOutput, calls=%fused_computation.19 | convolution fusion | flops 1664434176 | bytes 11304960 | tf_op jit(solution)/shard_map/rd,rf->df/dot_general | solution.py:71
  210.7 84.0 %reduce-scatter.7.cloned.1.call-done = bf16[1,8,33,384]{3,1,2,0:T(8,128)(2,1)} async-done(((bf16[16,8,33,384]{3,1,2,0:T(8,128)(2,1)}), bf16[1,8,33,384]{3,1,2,0:T(8,128)(2,1)}) %reduce-scatter.7.cloned.1.call-update) | async-done | bytes 202768
  294.7 1.3 multiply_reduce_fusion
  296.0 0.1 copy.61
  296.1 1.0 pad_maximum_fusion.2
  297.1 0.8 copy.53
  297.9 4.8 %all-to-all-start.1 = ((bf16[1,8,33,512]{3,2,0,1:T(8,128)(2,1)}), bf16[1,8,33,512]{3,2,0,1:T(8,128)(2,1)S(1)}, u32[]{:S(2)}, u32[]{:S(2)}) async-start(bf16[1,8,33,512]{3,2,0,1:T(8,128)(2,1)} %copy.53), calls=%async_computation.2 | async-start | bytes 655360 | tf_op jit(solution)/shard_map/all_to_all | solution.py:94
  302.7 6.2 %fusion.21 = bf16[1,256,3072]{2,1,0:T(8,128)(2,1)} fusion(bf16[1056,256]{1,0:T(8,128)(2,1)S(1)} %get-tuple-element.37, bf16[1056,6144]{1,0:T(8,128)(2,1)} %reshape.90), kind=kOutput, calls=%fused_computation.17 | convolution fusion | flops 1661730816 | bytes 8601600 | tf_op jit(solution)/shard_map/rf,rd->fd/dot_general | solution.py:64
  309.1 1.1 convolution_convert_fusion.4
  310.1 0.2 fusion.37
  310.4 0.1 add.51
  310.4 2.0 gather_fusion
  312.4 0.1 reshape.96
  312.5 0.6 copy.55
  (47 shorter events, 0.7 us)
Async XLA Ops:
  7.2 153.3 %copy-start = (bf16[1,256,3072]{2,1,0:T(8,128)(2,1)S(1)}, bf16[1,256,3072]{2,1,0:T(8,128)(2,1)}, u32[]{:S(2)}) copy-start(bf16[1,256,3072]{2,1,0:T(8,128)(2,1)} %param.13) | copy-start | bytes 4718596
  7.2 6.4 %copy-start.3 = (bf16[128,384]{1,0:T(8,128)(2,1)S(1)}, bf16[128,384]{1,0:T(8,128)(2,1)}, u32[]{:S(2)}) copy-start(bf16[128,384]{1,0:T(8,128)(2,1)} %param.7) | copy-start | bytes 294916
  7.2 131.1 %all-gather.2.cloned.1.call-start = ((), (), s32[]{:S(2)}) async-start(), calls=%async_computation.4 | async-start | bytes 16220160 | tf_op jit(solution)/shard_map/all_gather | solution.py:46
  32.0 163.3 %reduce-scatter.5.cloned.1.call-start = ((), (), s32[]{:S(2)}) async-start(), calls=%async_computation.5 | async-start | bytes 9732096 | tf_op jit(solution)/shard_map/reduce_scatter | solution.py:82
  150.1 7.0 %copy-start.2 = (bf16[1056,6144]{1,0:T(8,128)(2,1)S(1)}, bf16[1056,6144]{1,0:T(8,128)(2,1)}, u32[]{:S(2)}) copy-start(bf16[1056,6144]{1,0:T(8,128)(2,1)} %reshape.90) | copy-start | bytes 38928388
  150.1 7.4 %copy-start.4 = (bf16[1,3072,256]{2,1,0:T(8,128)(2,1)S(1)}, bf16[1,3072,256]{2,1,0:T(8,128)(2,1)}, u32[]{:S(2)}) copy-start(bf16[1,3072,256]{2,1,0:T(8,128)(2,1)} %param.12) | copy-start | bytes 4718596
  157.5 2.9 copy-start.5
  167.3 127.4 %reduce-scatter.7.cloned.1.call-start = ((), (), s32[]{:S(2)}) async-start(), calls=%async_computation.6 | async-start | bytes 3446784
  195.6 4.9 %copy-start.6 = (f32[1056,256]{1,0:T(8,128)S(1)}, f32[1056,256]{1,0:T(8,128)}, u32[]{:S(2)}) copy-start(f32[1056,256]{1,0:T(8,128)} %copy-done.5) | copy-start | bytes 3244036
  195.6 11.5 %slice-start = ((s8[12976128]{0:T(1024)(128)(4,1)}), s8[4194304]{0:T(1024)(128)(4,1)S(1)}, s32[]{:S(2)}) async-start(s8[12976128]{0:T(1024)(128)(4,1)} %bitcast.79), calls=%async_computation.7 | async-start | bytes 8388608
  195.6 11.5 %slice-start.1 = ((s8[12976128]{0:T(1024)(128)(4,1)}), s8[4194304]{0:T(1024)(128)(4,1)S(1)}, s32[]{:S(2)}) async-start(s8[12976128]{0:T(1024)(128)(4,1)} %bitcast.79), calls=%async_computation.8 | async-start | bytes 8388608
  200.5 6.6 %slice-start.2 = ((s8[12976128]{0:T(1024)(128)(4,1)}), s8[4194304]{0:T(1024)(128)(4,1)S(1)}, s32[]{:S(2)}) async-start(s8[12976128]{0:T(1024)(128)(4,1)} %bitcast.79), calls=%async_computation.9 | async-start | bytes 8388608
  200.5 6.5 %slice-start.3 = ((s8[12976128]{0:T(1024)(128)(4,1)}), s8[393216]{0:T(1024)(128)(4,1)S(1)}, s32[]{:S(2)}) async-start(s8[12976128]{0:T(1024)(128)(4,1)} %bitcast.79), calls=%async_computation.10 | async-start | bytes 786432
  200.5 6.5 %copy-start.7 = (f32[1056,256]{1,0:T(8,128)S(1)}, f32[1056,256]{1,0:T(8,128)}, u32[]{:S(2)}) copy-start(f32[1056,256]{1,0:T(8,128)} %get-tuple-element.38) | copy-start | bytes 3244036
  297.9 11.0 %all-to-all-start.1 = ((bf16[1,8,33,512]{3,2,0,1:T(8,128)(2,1)}), bf16[1,8,33,512]{3,2,0,1:T(8,128)(2,1)S(1)}, u32[]{:S(2)}, u32[]{:S(2)}) async-start(bf16[1,8,33,512]{3,2,0,1:T(8,128)(2,1)} %copy.53), calls=%async_computation.2 | async-start | bytes 655360 | tf_op jit(solution)/shard_map/all_to_all | solution.py:94
  310.4 2.7 copy-start.1
Sparse Core Ops, SparseCore 0:
  32.2 106.0 all-gather.1
  167.4 27.8 reduce-scatter.4
  198.9 95.6 reduce-scatter.6

commit v8 on v6

--- a/solution.py
+++ b/solution.py
@@ -47,21 +47,20 @@
     n_blk = blocks_all.shape[0]
     d_all = recv.shape[-1]
     n_rows = n_blk * capacity
-    flat_all = blocks_all.reshape(n_rows, 2 * d_all)
-    gathered = flat_all[:, :d_all]
-    grads_in = flat_all[:, d_all:]
+    gathered = blocks_all[:, :, :d_all]
+    grads_in = blocks_all[:, :, d_all:]
     gate_slab = w_gate[0]
     up_slab = w_up[0]
     down_slab = w_down[0]
 
-    gate_pre = jnp.dot(gathered, gate_slab, preferred_element_type=jnp.float32)
-    up_pre = jnp.dot(gathered, up_slab, preferred_element_type=jnp.float32)
+    gate_pre = jnp.einsum("gcd,df->gcf", gathered, gate_slab, preferred_element_type=jnp.float32)
+    up_pre = jnp.einsum("gcd,df->gcf", gathered, up_slab, preferred_element_type=jnp.float32)
     sigmoid_gate = jax.nn.sigmoid(gate_pre)
     hidden = (gate_pre * sigmoid_gate * up_pre).astype(jnp.bfloat16)
-    partial_out = jnp.dot(hidden, down_slab, preferred_element_type=jnp.float32).astype(jnp.bfloat16)
+    partial_out = jnp.einsum("gcf,fd->gcd", hidden, down_slab, preferred_element_type=jnp.float32).astype(jnp.bfloat16)
 
-    d_hidden = jnp.einsum("rd,fd->rf", grads_in, down_slab, preferred_element_type=jnp.float32)
-    d_down = jnp.einsum("rf,rd->fd", hidden, grads_in, preferred_element_type=jnp.float32).astype(
+    d_hidden = jnp.einsum("gcd,fd->gcf", grads_in, down_slab, preferred_element_type=jnp.float32)
+    d_down = jnp.einsum("gcf,gcd->fd", hidden, grads_in, preferred_element_type=jnp.float32).astype(
         jnp.bfloat16
     )
     d_gate_act = (
@@ -69,9 +68,9 @@
     ).astype(jnp.bfloat16)
     d_up_act = (d_hidden * gate_pre * sigmoid_gate).astype(jnp.bfloat16)
     d_gate = jnp.einsum(
-        "rd,rf->df", gathered, d_gate_act, preferred_element_type=jnp.float32
+        "gcd,gcf->df", gathered, d_gate_act, preferred_element_type=jnp.float32
     ).astype(jnp.bfloat16)
-    d_up = jnp.einsum("rd,rf->df", gathered, d_up_act, preferred_element_type=jnp.float32).astype(
+    d_up = jnp.einsum("gcd,gcf->df", gathered, d_up_act, preferred_element_type=jnp.float32).astype(
         jnp.bfloat16
     )
 

time: 307 us -> 522 us (1.70)
  waiting for transfers between devices: 205 us -> 408 us
  matrix products: 35.2 us -> 41.9 us
    unnamed x3, waiting for transfers between devices: 98.7 us -> 302 us
    dot_general x7, matrix products: 31.6 us -> 38.3 us  [the longest x1 6.97 us: local(): jnp.einsum('gcd,gcf->df', gathered, d_up_act, preferred_element_type=jnp....]
    reshape x1 -> x2, local copies, waits for them, and re-layouts: 11.8 us -> 17.5 us  [local(): partial_out.reshape(n_blk, capacity, experts, d_all // experts)]
  transfers between devices with their start and end apart: 3 -> 3, of which waited for: 2 -> 2; matrix products, arithmetic and copies ran while one was open for 7% -> 5% of each run, Pallas kernels for 0% -> 0%
where the time goes in v8:
time: 522 us; the launch traced here: 521 us
  waiting for transfers between devices  408 us (78%)
  matrix products  41.9 us (8%)
  local copies, waits for them, and re-layouts  28.3 us (5%)
  blocking collectives  16.7 us (3%)
  between operations  14.4 us (3%)
  starting transfers between devices  7.75 us (1%)
    unnamed x3, waiting for transfers between devices  302 us
    all_gather x1, waiting for transfers between devices, local(): blocks_all = lax.all_gather(both, DP, axis=0, tiled=True)  106 us
    reshape x2, local copies, waits for them, and re-layouts, local(): partial_out.reshape(n_blk, capacity, experts, d_all // experts)  17.5 us
    all_to_all x1, blocking collectives, local(): lax.all_to_all(sent, 'expert', split_axis=1, concat_axis=3, tiled=True)  16.7 us
  transfers between devices with their start and end apart: 3, of which 2 were waited for; matrix products, arithmetic and copies ran while one was open for 5% of the time, Pallas kernels for 0%

profile of v8, /device:TPU:2, one launch (start us, length us, event | category | flops | bytes accessed | tf_op | source)
XLA Modules:
  0.0 521.5 jit_solution(15243658312552281904)
XLA Ops:
  7.2 0.9 copy.74
  8.1 0.1 eq.67
  8.3 0.1 eq.63
  8.4 0.8 slice_bitcast_fusion.3
  9.2 0.6 reduce-window.6
  9.8 0.2 slice_reduce_fusion
  10.0 0.1 fusion.61
  10.1 0.1 reshape.77
  10.3 0.7 compare_select_fusion
  11.0 1.1 convolution_convert_fusion.3
  12.1 0.1 reshape.78
  12.2 1.1 convolution_convert_fusion.1
  13.3 0.1 reshape.80
  13.4 0.4 convolution_convert_fusion.2
  13.9 0.1 pad_maximum_fusion
  14.1 16.7 %all_to_all.27 = bf16[3,8,33,384]{3,2,0,1:T(8,128)(2,1)S(1)} all-to-all(bf16[3,8,33,384]{3,2,0,1:T(8,128)(2,1)S(1)} %copy.77), channel_id=1, replica_groups=mesh['dpo'=16,'core'=2,'expert'=8] {'expert'}, dimensions={1} | all-to-all | bytes 1216512 | tf_op jit(solution)/shard_map/all_to_all | solution.py:43
  30.9 0.1 squeeze.21
  31.1 0.1 squeeze.22
  31.2 0.8 pad_maximum_fusion.1
  32.1 106.2 %all-gather.2.cloned.1.call-done = bf16[32,33,6144]{2,1,0:T(8,128)(2,1)} async-done(((bf16[1,33,6144]{2,1,0:T(8,128)(2,1)}), bf16[32,33,6144]{2,1,0:T(8,128)(2,1)}) %all-gather.2.cloned.1.call-update) | async-done | bytes 12976144 | tf_op jit(solution)/shard_map/all_gather | solution.py:46
  138.3 6.1 %fusion.10 = f32[32,33,256]{2,1,0:T(8,128)S(1)} fusion(bf16[32,33,6144]{2,1,0:T(8,128)(2,1)} %all-gather.2.cloned.1.call-done, bf16[1,3072,256]{2,1,0:T(8,128)(2,1)} %param.11), kind=kOutput, calls=%fused_computation.13 | convolution fusion | flops 1660944384 | bytes 10518528 | tf_op jit(solution)/shard_map/gcd,df->gcf/dot_general | solution.py:56
  144.4 2.1 copy-done.2
  146.4 0.4 copy-done.3
  146.8 3.7 multiply_convert_fusion.2
  150.5 5.4 %convolution_convert_fusion = bf16[32,33,3072]{2,1,0:T(8,128)(2,1)} fusion(bf16[32,33,256]{2,1,0:T(8,128)(2,1)S(1)} %get-tuple-element.49, bf16[1,256,3072]{2,1,0:T(8,128)(2,1)S(1)} %copy-done), kind=kOutput, calls=%fused_computation.6 | convolution fusion | flops 1664188416 | bytes 8601600 | tf_op jit(solution)/shard_map/gcf,fd->gcd/dot_general | solution.py:60
  155.9 10.8 %reshape.102 = bf16[32,33,8,384]{3,2,1,0:T(8,128)(2,1)} reshape(bf16[32,33,3072]{2,1,0:T(8,128)(2,1)} %convolution_convert_fusion) | data formatting | bytes 12976128 | tf_op jit(solution)/shard_map/reshape | solution.py:77
  166.7 6.7 %copy.100 = bf16[32,33,8,384]{3,2,0,1:T(8,128)(2,1)} copy(bf16[32,33,8,384]{3,2,1,0:T(8,128)(2,1)} %reshape.102) | data formatting | bytes 12976128 | tf_op jit(solution)/shard_map/reshape | solution.py:77
  173.4 0.1 copy.86
  173.5 0.1 reshape.85
  173.7 0.4 copy-done.4
  174.1 0.6 dynamic-slice
  174.6 5.7 %fusion.2 = f32[32,33,256]{2,1,0:T(8,128)S(1)} fusion(bf16[32,33,6144]{2,1,0:T(8,128)(2,1)} %all-gather.2.cloned.1.call-done, bf16[1,256,3072]{2,1,0:T(8,128)(2,1)S(1)} %copy-done), kind=kOutput, calls=%fused_computation.3 | convolution fusion | flops 1660944384 | bytes 10518528 | tf_op jit(solution)/shard_map/gcd,fd->gcf/dot_general | solution.py:62
  180.4 7.0 %fusion.33 = bf16[1,3072,256]{2,1,0:T(8,128)(2,1)} fusion(bf16[32,33,6144]{2,1,0:T(8,128)(2,1)} %all-gather.2.cloned.1.call-done, f32[32,33,256]{2,1,0:T(8,128)S(1)} %fusion.2, f32[32,33,256]{2,1,0:T(8,128)S(1)} %copy-done.6), kind=kOutput, calls=%fused_computation.22 | convolution fusion | flops 1663352832 | bytes 11599872 | tf_op jit(solution)/shard_map/gcd,gcf->df/dot_general | solution.py:73
  187.5 3.8 fusion.30
  191.3 301.7 %all-reduce.4.cloned.1.call-done = bf16[32,8,33,384]{3,1,0,2:T(8,128)(2,1)} async-done(((bf16[32,8,33,384]{3,1,0,2:T(8,128)(2,1)}), bf16[32,8,33,384]{3,1,0,2:T(8,128)(2,1)}) %all-reduce.4.cloned.1.call-update) | async-done | bytes 6488080
  493.0 1.9 multiply_reduce_fusion
  494.9 0.1 copy.96
  495.1 0.8 copy.82
  495.9 7.7 %all-to-all-start.1 = ((bf16[1,8,33,512]{3,2,0,1:T(8,128)(2,1)}), bf16[1,8,33,512]{3,2,0,1:T(8,128)(2,1)S(1)}, u32[]{:S(2)}, u32[]{:S(2)}) async-start(bf16[1,8,33,512]{3,2,0,1:T(8,128)(2,1)} %copy.82), calls=%async_computation.1 | async-start | bytes 655360 | tf_op jit(solution)/shard_map/all_to_all | solution.py:89
  503.6 6.6 %fusion.36 = bf16[1,256,3072]{2,1,0:T(8,128)(2,1)} fusion(bf16[32,33,256]{2,1,0:T(8,128)(2,1)S(1)} %get-tuple-element.49, bf16[32,33,6144]{2,1,0:T(8,128)(2,1)} %all-gather.2.cloned.1.call-done), kind=kOutput, calls=%fused_computation.23 | convolution fusion | flops 1661730816 | bytes 9977856 | tf_op jit(solution)/shard_map/gcf,gcd->fd/dot_general | solution.py:63
  510.2 0.1 copy.101
  510.3 0.1 slice_add_fusion
  510.5 0.1 copy.85
  510.6 0.1 add.49
  510.8 1.1 convolution_convert_fusion.4
  511.9 1.9 gather_fusion
  513.9 0.1 reshape.84
  514.0 0.6 copy.87
  (47 shorter events, 0.8 us)
Async XLA Ops:
  7.2 143.3 %copy-start = (bf16[1,256,3072]{2,1,0:T(8,128)(2,1)S(1)}, bf16[1,256,3072]{2,1,0:T(8,128)(2,1)}, u32[]{:S(2)}) copy-start(bf16[1,256,3072]{2,1,0:T(8,128)(2,1)} %param.13) | copy-start | bytes 4718596
  7.2 6.2 %copy-start.1 = (bf16[128,384]{1,0:T(8,128)(2,1)S(1)}, bf16[128,384]{1,0:T(8,128)(2,1)}, u32[]{:S(2)}) copy-start(bf16[128,384]{1,0:T(8,128)(2,1)} %param.8) | copy-start | bytes 294916
  7.2 131.1 %all-gather.2.cloned.1.call-start = ((), (), s32[]{:S(2)}) async-start(), calls=%async_computation.2 | async-start | bytes 16220160 | tf_op jit(solution)/shard_map/all_gather | solution.py:46
  32.0 460.9 %all-reduce.4.cloned.1.call-start = ((), (), s32[]{:S(2)}) async-start(), calls=%async_computation.3 | async-start | bytes 12976128
  138.3 8.2 %copy-start.2 = (bf16[32,33,6144]{2,1,0:T(8,128)(2,1)S(1)}, bf16[32,33,6144]{2,1,0:T(8,128)(2,1)}, u32[]{:S(2)}) copy-start(bf16[32,33,6144]{2,1,0:T(8,128)(2,1)} %all-gather.2.cloned.1.call-done) | copy-start | bytes 38928388
  138.3 8.6 %copy-start.3 = (bf16[1,3072,256]{2,1,0:T(8,128)(2,1)S(1)}, bf16[1,3072,256]{2,1,0:T(8,128)(2,1)}, u32[]{:S(2)}) copy-start(bf16[1,3072,256]{2,1,0:T(8,128)(2,1)} %param.12) | copy-start | bytes 4718596
  146.8 3.7 copy-start.5
  173.4 0.7 copy-start.4
  174.6 5.8 %copy-start.6 = (f32[32,33,256]{2,1,0:T(8,128)S(1)}, f32[32,33,256]{2,1,0:T(8,128)}, u32[]{:S(2)}) copy-start(f32[32,33,256]{2,1,0:T(8,128)} %copy-done.5) | copy-start | bytes 3244036
  174.6 12.8 %slice-start = ((s8[15728640]{0:T(1024)(128)(4,1)}), s8[4194304]{0:T(1024)(128)(4,1)S(1)}, s32[]{:S(2)}) async-start(s8[15728640]{0:T(1024)(128)(4,1)} %bitcast.104), calls=%async_computation.4 | async-start | bytes 8388608
  180.4 7.0 %slice-start.1 = ((s8[15728640]{0:T(1024)(128)(4,1)}), s8[4194304]{0:T(1024)(128)(4,1)S(1)}, s32[]{:S(2)}) async-start(s8[15728640]{0:T(1024)(128)(4,1)} %bitcast.104), calls=%async_computation.5 | async-start | bytes 8388608
  180.4 7.0 %slice-start.2 = ((s8[15728640]{0:T(1024)(128)(4,1)}), s8[4194304]{0:T(1024)(128)(4,1)S(1)}, s32[]{:S(2)}) async-start(s8[15728640]{0:T(1024)(128)(4,1)} %bitcast.104), calls=%async_computation.6 | async-start | bytes 8388608
  180.4 7.0 %slice-start.3 = ((s8[15728640]{0:T(1024)(128)(4,1)}), s8[3145728]{0:T(1024)(128)(4,1)S(1)}, s32[]{:S(2)}) async-start(s8[15728640]{0:T(1024)(128)(4,1)} %bitcast.104), calls=%async_computation.7 | async-start | bytes 6291456
  180.4 7.0 %copy-start.7 = (f32[32,33,256]{2,1,0:T(8,128)S(1)}, f32[32,33,256]{2,1,0:T(8,128)}, u32[]{:S(2)}) copy-start(f32[32,33,256]{2,1,0:T(8,128)} %get-tuple-element.50) | copy-start | bytes 3244036
  495.9 14.3 %all-to-all-start.1 = ((bf16[1,8,33,512]{3,2,0,1:T(8,128)(2,1)}), bf16[1,8,33,512]{3,2,0,1:T(8,128)(2,1)S(1)}, u32[]{:S(2)}, u32[]{:S(2)}) async-start(bf16[1,8,33,512]{3,2,0,1:T(8,128)(2,1)} %copy.82), calls=%async_computation.1 | async-start | bytes 655360 | tf_op jit(solution)/shard_map/all_to_all | solution.py:89
Sparse Core Ops, SparseCore 0:
  32.1 106.0 all-gather.1
  173.5 319.3 all-reduce.3
